TPU v7x, 1024 devices: a whole 8x8x8 slice. The times are simulated.
1024 devices in a mesh: dp: 8 (over x), ctx: 16 (over y, core), tp: 8 (over z).
Axes of the slice: x: 8, y: 8, z: 8, core: 2. Of those that a mesh axis runs over, the one named last changes fastest.
Arguments:
- query_rows: bfloat16 [8, 6144, 8192], P('dp', 'ctx', 'tp'), may hold values from -2.5 to 2.5
- key_rows: bfloat16 [8, 6144, 1024], P('dp', 'ctx', 'tp'), may hold values from -2.5 to 2.5
- value_rows: bfloat16 [8, 6144, 1024], P('dp', 'ctx', 'tp'), may hold values from -6 to 6
- out_grad: bfloat16 [8, 6144, 8192], P('dp', 'ctx', 'tp'), may hold values from -6 to 6
- assistant: int32 [8, 48], P('dp'), may hold values from 0 to 1, as said below
- turn_first: int32 [8, 48], P('dp'), may hold values from 0 to 47, as said below
Outputs:
- query_grad: bfloat16 [8, 6144, 8192], P('dp', 'ctx', 'tp')
- key_grad: bfloat16 [8, 6144, 1024], P('dp', 'ctx', 'tp')
- value_grad: bfloat16 [8, 6144, 1024], P('dp', 'ctx', 'tp')
Inputs may be any that keep to these rules, and one draw needn't show every extreme that they name: Among the 3 blocks at positions d * 3 to d * 3 + 2 at most 2 are assistant blocks, and in every sequence some such group holds exactly 2. Turns are runs of whole blocks: turn_first never falls, equals the block's own index where a turn begins, and q - 4 <= turn_first[q] <= q; in every sequence some block has q - turn_first[q] = 4.
All inputs are finite; a program needn't handle non-finite values.
Results may differ from a plain program's by a relative error of at most 0.005.
Values may be sent and summed in bfloat16 or wider, within the bound.
A program may use at most 32 MiB of HBM per device.

v0:
```python
import math

import jax
import jax.numpy as jnp
from jax import lax
from jax.sharding import PartitionSpec as P

BLK = 128


def shifted(block, axis, distance):
    devices = range(lax.axis_size(axis))
    route = [(i - distance, i) for i in devices if i - distance in devices]
    return lax.ppermute(block, axis, route)


def per_device(query_rows, key_rows, value_rows, out_grad, assistant, turn_first):
    token_count = query_rows.shape[1]
    head_width = key_rows.shape[2]
    head_count = query_rows.shape[2] // head_width
    block_count = token_count // BLK
    far_blocks = block_count // 2
    reach_blocks = block_count + far_blocks
    slot_count = (block_count + 1) // 2
    key_span = (reach_blocks + 1) * BLK
    far_rows = far_blocks * BLK
    window_blocks = reach_blocks + block_count
    scale_factor = 1.0 / math.sqrt(head_width)
    ctx_rank = lax.axis_index("ctx")
    block_base = ctx_rank * block_count
    assist_local = lax.dynamic_slice_in_dim(assistant[0], block_base, block_count)
    start_local = lax.dynamic_slice_in_dim(turn_first[0], block_base, block_count)
    key_local = key_rows[0]
    value_local = value_rows[0]
    fetched = []
    for distance in (1, 2):
        fetched.append(shifted((key_local, value_local), "ctx", distance))
    far_keys = fetched[1][0][token_count - far_rows :]
    far_values = fetched[1][1][token_count - far_rows :]
    window_keys = jnp.concatenate([far_keys, fetched[0][0], key_local], 0)
    window_values = jnp.concatenate([far_values, fetched[0][1], value_local], 0)
    block_ids = jnp.arange(block_count, dtype=jnp.int32)
    order_pos = jnp.cumsum(assist_local) - 1
    picked = (assist_local[None, :] == 1) & (
        order_pos[None, :] == jnp.arange(slot_count, dtype=jnp.int32)[:, None]
    )
    slot_block = jnp.sum(jnp.where(picked, block_ids[None, :], 0), axis=1)
    slot_live = jnp.any(picked, axis=1)
    query_blocks = query_rows[0].reshape(block_count, BLK, head_count, head_width)
    grad_blocks = out_grad[0].reshape(block_count, BLK, head_count, head_width)

    def slot_grads(slot_args):
        block_index, alive = slot_args
        query_block = lax.dynamic_index_in_dim(query_blocks, block_index, 0, keepdims=False)
        grad_block = jnp.where(
            alive,
            lax.dynamic_index_in_dim(grad_blocks, block_index, 0, keepdims=False),
            jnp.zeros((), grad_blocks.dtype),
        )
        key_window = lax.dynamic_slice_in_dim(window_keys, block_index * BLK, key_span, 0)
        value_window = lax.dynamic_slice_in_dim(window_values, block_index * BLK, key_span, 0)
        scores = jnp.einsum(
            "bhd,kd->hbk", query_block, key_window, preferred_element_type=jnp.float32
        )
        key_pos = (block_base + block_index - reach_blocks) * BLK + jnp.arange(
            key_span, dtype=jnp.int32
        )
        query_pos = (block_base + block_index) * BLK + jnp.arange(BLK, dtype=jnp.int32)
        turn_begin = lax.dynamic_index_in_dim(start_local, block_index, 0, keepdims=False) * BLK
        allowed = (key_pos[None, :] >= turn_begin) & (key_pos[None, :] <= query_pos[:, None])
        weights = jnp.where(allowed[None], jnp.exp(scores * scale_factor), 0.0)
        attention = weights / jnp.sum(weights, axis=2, keepdims=True)
        prob_grad = jnp.einsum(
            "bhd,kd->hbk", grad_block, value_window, preferred_element_type=jnp.float32
        )
        row_delta = jnp.sum(attention * prob_grad, axis=2, keepdims=True)
        score_grad = (attention * (prob_grad - row_delta)).astype(jnp.bfloat16)
        attention_low = attention.astype(jnp.bfloat16)
        query_part = (
            scale_factor
            * jnp.einsum("hbk,kd->bhd", score_grad, key_window, preferred_element_type=jnp.float32)
        ).astype(jnp.bfloat16)
        key_part = scale_factor * jnp.einsum(
            "hbk,bhd->kd", score_grad, query_block, preferred_element_type=jnp.float32
        )
        value_part = jnp.einsum(
            "hbk,bhd->kd", attention_low, grad_block, preferred_element_type=jnp.float32
        )
        return (query_part, key_part, value_part)

    slot_query, slot_key, slot_value = lax.map(slot_grads, (slot_block, slot_live))
    query_grad = (
        jnp.zeros((block_count, BLK, head_count, head_width), jnp.float32)
        .at[slot_block]
        .add(slot_query.astype(jnp.float32))
    )
    query_grad = query_grad.astype(jnp.bfloat16).reshape(1, token_count, head_count * head_width)
    placement = (
        slot_block[:, None, None] + jnp.arange(reach_blocks + 1, dtype=jnp.int32)[None, :, None]
        == jnp.arange(window_blocks, dtype=jnp.int32)[None, None, :]
    ).astype(jnp.float32)
    highest = lax.Precision.HIGHEST
    key_window_grad = jnp.einsum(
        "srw,srbd->wbd",
        placement,
        slot_key.reshape(slot_count, reach_blocks + 1, BLK, head_width),
        precision=highest,
    ).reshape(window_blocks * BLK, head_width)
    value_window_grad = jnp.einsum(
        "srw,srbd->wbd",
        placement,
        slot_value.reshape(slot_count, reach_blocks + 1, BLK, head_width),
        precision=highest,
    ).reshape(window_blocks * BLK, head_width)
    own_keys = key_window_grad[far_rows + token_count :]
    own_values = value_window_grad[far_rows + token_count :]
    near_keys = key_window_grad[far_rows : far_rows + token_count]
    near_values = value_window_grad[far_rows : far_rows + token_count]
    far_key_grad = key_window_grad[:far_rows]
    far_value_grad = value_window_grad[:far_rows]
    returned = []
    filler = jnp.zeros((token_count - far_rows, head_width), jnp.float32)
    for distance in (1, 2):
        if distance == 1:
            outgoing = (near_keys, near_values)
        else:
            outgoing = (
                jnp.concatenate([filler, far_key_grad], 0),
                jnp.concatenate([filler, far_value_grad], 0),
            )
        returned.append(shifted((outgoing[0], outgoing[1]), "ctx", -distance))
    key_total = own_keys + returned[0][0] + returned[1][0]
    value_total = own_values + returned[0][1] + returned[1][1]
    key_grad = key_total.astype(jnp.bfloat16)
    value_grad = value_total.astype(jnp.bfloat16)
    return (query_grad, key_grad[None], value_grad[None])


def solution(mesh):
    return jax.shard_map(
        per_device,
        mesh=mesh,
        in_specs=(
            P("dp", "ctx", "tp"),
            P("dp", "ctx", "tp"),
            P("dp", "ctx", "tp"),
            P("dp", "ctx", "tp"),
            P("dp", None),
            P("dp", None),
        ),
        out_specs=(P("dp", "ctx", "tp"), P("dp", "ctx", "tp"), P("dp", "ctx", "tp")),
        check_vma=False,
    )
```

profile of v0, /device:TPU:1, one launch (start us, length us, event | category | flops | bytes accessed | tf_op | source)
XLA Modules:
  0.0 72.9 jit_solution(2144468028544321887)
XLA Ops:
  0.6 0.0 copy-start
  0.6 0.0 copy-start.1
  0.7 0.0 copy-start.2
  0.7 4.8 %collective-permute-start.1 = (bf16[384,128]{1,0:T(8,128)(2,1)}, bf16[384,128]{1,0:T(8,128)(2,1)S(1)}, u32[]{:S(2)}, u32[]{:S(2)}) collective-permute-start(bf16[384,128]{1,0:T(8,128)(2,1)} %bitcast.183), channel_id=1, source_target_pairs={{0,8},{8,16},{16,24},{24,32},{32,40},{40,48},{48,56},{56,64},{64,7... | collective-permute-start | bytes 294920 | tf_op jit(solution)/shard_map/ppermute | solution.py:14
  5.5 3.3 %collective-permute-start = (bf16[384,128]{1,0:T(8,128)(2,1)}, bf16[384,128]{1,0:T(8,128)(2,1)S(1)}, u32[]{:S(2)}, u32[]{:S(2)}) collective-permute-start(bf16[384,128]{1,0:T(8,128)(2,1)} %bitcast.184), channel_id=1, source_target_pairs={{0,16},{8,24},{16,32},{24,40},{32,48},{40,56},{48,64},{56,72},{64,... | collective-permute-start | bytes 294920 | tf_op jit(solution)/shard_map/ppermute | solution.py:14
  8.8 2.2 %collective-permute-start.3 = (bf16[384,128]{1,0:T(8,128)(2,1)}, bf16[384,128]{1,0:T(8,128)(2,1)S(1)}, u32[]{:S(2)}, u32[]{:S(2)}) collective-permute-start(bf16[384,128]{1,0:T(8,128)(2,1)} %bitcast.186), channel_id=1, source_target_pairs={{0,8},{8,16},{16,24},{24,32},{32,40},{40,48},{48,56},{56,64},{64,7... | collective-permute-start | bytes 294920 | tf_op jit(solution)/shard_map/ppermute | solution.py:14
  11.0 3.3 %collective-permute-start.2 = (bf16[384,128]{1,0:T(8,128)(2,1)}, bf16[384,128]{1,0:T(8,128)(2,1)S(1)}, u32[]{:S(2)}, u32[]{:S(2)}) collective-permute-start(bf16[384,128]{1,0:T(8,128)(2,1)} %bitcast.187), channel_id=1, source_target_pairs={{0,16},{8,24},{16,32},{24,40},{32,48},{40,56},{48,64},{56,72},{64,... | collective-permute-start | bytes 294920 | tf_op jit(solution)/shard_map/ppermute | solution.py:14
  14.4 0.7 %compare_bitcast_fusion = pred[3]{0:T(512)(128)(4,1)S(1)} fusion(s32[1,48]{1,0:T(1,128)} %param.12, s32[]{:T(128)S(6)} %select_n.59), kind=kLoop, calls=%fused_computation.63 | loop fusion | flops 3 | bytes 19 | tf_op jit(solution)/shard_map/and | solution.py:44
  15.1 0.7 fusion.51
  15.8 0.2 reduce-window.8
  16.0 0.1 select_reduce_fusion
  16.1 0.6 fusion.49
  16.8 0.1 iota_add_fusion.2
  16.8 1.3 %copy.46 = bf16[48,8,8,128]{3,2,1,0:T(8,128)(2,1)S(1)} copy(bf16[48,8,8,128]{3,1,2,0:T(8,128)(2,1)} %bitcast.177) | data formatting | bytes 1572864
  18.1 1.3 %copy.47 = bf16[48,8,8,128]{3,2,1,0:T(8,128)(2,1)S(1)} copy(bf16[48,8,8,128]{3,1,2,0:T(8,128)(2,1)} %bitcast.178) | data formatting | bytes 1572864
  19.5 0.0 copy-done
  19.5 0.7 dynamic-slice_bitcast_fusion
  20.1 0.0 collective-permute-done
  20.2 0.0 collective-permute-done.2
  20.2 0.0 collective-permute-done.1
  20.2 0.0 copy-done.1
  20.2 0.0 collective-permute-done.3
  20.3 26.1 %while.16 = (s32[]{:T(128)}, bf16[2,128,8,128]{1,3,2,0:T(8,128)(2,1)}, f32[2,640,128]{2,1,0:T(8,128)S(1)}, f32[2,640,128]{2,1,0:T(8,128)S(1)}, s32[2]{0:T(128)S(...) while((s32[]{:T(128)}, ...), condition=%wide.region_6.7_spmd, body=%wide.region_3.6_spmd.sunk | while | flops 851427328 | bytes 23608972 | solution.py:91
  20.3 0.6 dynamic_slice.92
  24.1 1.3 %dynamic_slice.93 = s32[1]{0:T(128)} dynamic-slice(s32[3]{0:T(128)} %get-tuple-element.345, s32[]{:T(128)S(6)} %select_n.108), dynamic_slice_sizes={1} | dynamic-slice | bytes 12 | tf_op jit(solution)/shard_map/while/body/eval_jaxpr/jit(dynamic_index_in_dim)/dynamic_slice | solution.py:69
  26.0 1.2 %dynamic_slice.94 = pred[1]{0:T(512)(128)(4,1)} dynamic-slice(pred[2]{0:T(512)(128)(4,1)} %get-tuple-element.348, s32[]{:T(128)S(6)} %copy.79), dynamic_slice_sizes={1} | dynamic-slice | bytes 6 | tf_op jit(solution)/shard_map/while/body/jit(dynamic_index_in_dim)/dynamic_slice | solution.py:91
  27.3 0.2 compare_and_fusion.3
  27.6 0.7 fusion.72
  28.2 1.3 %fusion.77 = f32[2,640,128]{2,1,0:T(8,128)S(1)} fusion(f32[2,640,128]{2,1,0:T(8,128)S(1)} %get-tuple-element.322, s32[]{:T(128)S(6)} %copy.79, bf16[1,128,8,128]{3,2,1,0:T(8,128)(2,1)S(1)} %get-tuple-element.297, pred[]{:T(512)} %bitcast.172, f32[640,128,8]{1,0,2:T(8,128)S(1)} %get-tuple-element.296, f32[8,128]{1,0:T(8,128)S(1)} %get-tuple-element.295, ...), kind=kOutput, calls=%fused_computation.14.clone.1 | convolution fusion | flops 170524672 | bytes 3297285 | tf_op jit(solution)/shard_map/while/body/eval_jaxpr/hbk,bhd->kd/dot_general | solution.py:86
  29.6 1.4 %fusion.73 = (f32[8,128]{1,0:T(8,128)S(1)}, f32[640,128,8]{1,0,2:T(8,128)S(1)}) fusion(f32[8,128]{1,0:T(8,128)S(1)} %get-tuple-element.295, f32[640,128,8]{1,0,2:T(8,128)S(1)} %get-tuple-element.296, pred[128,640]{0,1:T(8,128)(4,1)S(1)} %compare_and_fusion.3, bf16[1,128,8,128]{3,2,1,0:T(8,128)(2,1)S(1)} %get-tuple-element.297, pred[]{:T(512)} %bitcast.172, ...), kind=kOutput, calls=%fused_computation.3.clone.1 | convolution fusion | flops 171179008 | bytes 5758981 | tf_op jit(solution)/shard_map/while/body/eval_jaxpr/bhd,kd->hbk/dot_general | solution.py:73
  31.0 0.7 fusion.74
  31.7 0.5 fusion.76
  32.2 1.1 %fusion.75 = bf16[2,128,8,128]{1,3,2,0:T(8,128)(2,1)} fusion(bf16[2,128,8,128]{1,3,2,0:T(8,128)(2,1)} %get-tuple-element.320, s32[]{:T(128)S(6)} %copy.79, bf16[8,128,640]{1,2,0:T(8,128)(2,1)S(1)} %fusion.74, bf16[896,128]{1,0:T(8,128)(2,1)S(1)} %get-tuple-element.343, s32[]{:T(128)S(6)} %select_n.109), kind=kOutput, calls=%fused_computation.20.clone.1 | convolution fusion | flops 168034304 | bytes 1736712 | tf_op jit(solution)/shard_map/while/body/eval_jaxpr/hbk,kd->bhd/dot_general | solution.py:81
  33.3 0.6 dynamic_slice.92
  37.1 1.3 %dynamic_slice.93 = s32[1]{0:T(128)} dynamic-slice(s32[3]{0:T(128)} %get-tuple-element.345, s32[]{:T(128)S(6)} %select_n.108), dynamic_slice_sizes={1} | dynamic-slice | bytes 12 | tf_op jit(solution)/shard_map/while/body/eval_jaxpr/jit(dynamic_index_in_dim)/dynamic_slice | solution.py:69
  39.1 1.2 %dynamic_slice.94 = pred[1]{0:T(512)(128)(4,1)} dynamic-slice(pred[2]{0:T(512)(128)(4,1)} %get-tuple-element.348, s32[]{:T(128)S(6)} %copy.79), dynamic_slice_sizes={1} | dynamic-slice | bytes 6 | tf_op jit(solution)/shard_map/while/body/jit(dynamic_index_in_dim)/dynamic_slice | solution.py:91
  40.3 0.2 compare_and_fusion.3
  40.6 0.7 fusion.72
  41.3 1.3 %fusion.77 = f32[2,640,128]{2,1,0:T(8,128)S(1)} fusion(f32[2,640,128]{2,1,0:T(8,128)S(1)} %get-tuple-element.322, s32[]{:T(128)S(6)} %copy.79, bf16[1,128,8,128]{3,2,1,0:T(8,128)(2,1)S(1)} %get-tuple-element.297, pred[]{:T(512)} %bitcast.172, f32[640,128,8]{1,0,2:T(8,128)S(1)} %get-tuple-element.296, f32[8,128]{1,0:T(8,128)S(1)} %get-tuple-element.295, ...), kind=kOutput, calls=%fused_computation.14.clone.1 | convolution fusion | flops 170524672 | bytes 3297285 | tf_op jit(solution)/shard_map/while/body/eval_jaxpr/hbk,bhd->kd/dot_general | solution.py:86
  42.6 1.4 %fusion.73 = (f32[8,128]{1,0:T(8,128)S(1)}, f32[640,128,8]{1,0,2:T(8,128)S(1)}) fusion(f32[8,128]{1,0:T(8,128)S(1)} %get-tuple-element.295, f32[640,128,8]{1,0,2:T(8,128)S(1)} %get-tuple-element.296, pred[128,640]{0,1:T(8,128)(4,1)S(1)} %compare_and_fusion.3, bf16[1,128,8,128]{3,2,1,0:T(8,128)(2,1)S(1)} %get-tuple-element.297, pred[]{:T(512)} %bitcast.172, ...), kind=kOutput, calls=%fused_computation.3.clone.1 | convolution fusion | flops 171179008 | bytes 5758981 | tf_op jit(solution)/shard_map/while/body/eval_jaxpr/bhd,kd->hbk/dot_general | solution.py:73
  44.1 0.7 fusion.74
  44.8 0.5 fusion.76
  45.3 1.1 %fusion.75 = bf16[2,128,8,128]{1,3,2,0:T(8,128)(2,1)} fusion(bf16[2,128,8,128]{1,3,2,0:T(8,128)(2,1)} %get-tuple-element.320, s32[]{:T(128)S(6)} %copy.79, bf16[8,128,640]{1,2,0:T(8,128)(2,1)S(1)} %fusion.74, bf16[896,128]{1,0:T(8,128)(2,1)S(1)} %get-tuple-element.343, s32[]{:T(128)S(6)} %select_n.109), kind=kOutput, calls=%fused_computation.20.clone.1 | convolution fusion | flops 168034304 | bytes 1736712 | tf_op jit(solution)/shard_map/while/body/eval_jaxpr/hbk,kd->bhd/dot_general | solution.py:81
  46.4 1.1 %convolution_bitcast_fusion.2 = f32[7,128,128]{2,0,1:T(8,128)S(1)} fusion(f32[2,5,128,128]{3,2,1,0:T(8,128)S(1)} %bitcast.176, s32[2,5]{1,0:T(2,128)S(1)} %iota_add_fusion.2), kind=kOutput, calls=%fused_computation.46 | convolution fusion | flops 13762630 | bytes 1114152 | tf_op jit(solution)/shard_map/srw,srbd->wbd/dot_general | solution.py:103
  47.6 0.1 fusion.53
  47.7 1.1 %convolution_bitcast_fusion.1 = f32[7,128,128]{2,0,1:T(8,128)S(1)} fusion(f32[2,5,128,128]{3,2,1,0:T(8,128)S(1)} %bitcast.175, s32[2,5]{1,0:T(2,128)S(1)} %iota_add_fusion.2), kind=kOutput, calls=%fused_computation.45 | convolution fusion | flops 13762630 | bytes 1114152 | tf_op jit(solution)/shard_map/srw,srbd->wbd/dot_general | solution.py:109
  49.0 7.7 %collective-permute-start.4 = (f32[384,128]{1,0:T(8,128)S(1)}, f32[384,128]{1,0:T(8,128)}, u32[]{:S(2)}, u32[]{:S(2)}) collective-permute-start(f32[384,128]{1,0:T(8,128)S(1)} %bitcast.181), channel_id=1, source_target_pairs={{8,0},{16,8},{24,16},{32,24},{40,32},{48,40},{56,48},{64,56},{72,6... | collective-permute-start | bytes 589832 | tf_op jit(solution)/shard_map/ppermute | solution.py:14
  56.7 0.7 concatenate.14
  57.4 1.3 %collective-permute-start.5 = (f32[384,128]{1,0:T(8,128)}, f32[384,128]{1,0:T(8,128)}, u32[]{:S(2)}, u32[]{:S(2)}) collective-permute-start(f32[384,128]{1,0:T(8,128)} %concatenate.14), channel_id=1, source_target_pairs={{16,0},{24,8},{32,16},{40,24},{48,32},{56,40},{64,48},{72,56},{80,... | collective-permute-start | bytes 589832 | tf_op jit(solution)/shard_map/ppermute | solution.py:14
  58.6 0.1 fusion.52
  58.8 0.7 concatenate.15
  59.5 1.9 %collective-permute-start.6 = (f32[384,128]{1,0:T(8,128)S(1)}, f32[384,128]{1,0:T(8,128)}, u32[]{:S(2)}, u32[]{:S(2)}) collective-permute-start(f32[384,128]{1,0:T(8,128)S(1)} %bitcast.182), channel_id=1, source_target_pairs={{8,0},{16,8},{24,16},{32,24},{40,32},{48,40},{56,48},{64,56},{72,6... | collective-permute-start | bytes 589832 | tf_op jit(solution)/shard_map/ppermute | solution.py:14
  61.4 1.3 %collective-permute-start.7 = (f32[384,128]{1,0:T(8,128)}, f32[384,128]{1,0:T(8,128)}, u32[]{:S(2)}, u32[]{:S(2)}) collective-permute-start(f32[384,128]{1,0:T(8,128)} %concatenate.15), channel_id=1, source_target_pairs={{16,0},{24,8},{32,16},{40,24},{48,32},{56,40},{64,48},{72,56},{80,... | collective-permute-start | bytes 589832 | tf_op jit(solution)/shard_map/ppermute | solution.py:14
  62.7 1.3 %copy.32 = f32[2,128,8,128]{3,2,1,0:T(8,128)S(1)} copy(bf16[2,128,8,128]{1,3,2,0:T(8,128)(2,1)} %get-tuple-element.154) | data formatting | bytes 1572864 | tf_op jit(solution)/shard_map/convert_element_type | solution.py:95
  64.0 0.1 broadcast_in_dim.85
  64.2 1.0 %scatter_fusion = f32[3,128,8,128]{3,2,1,0:T(8,128)S(1)} fusion(f32[3,128,8,128]{3,2,1,0:T(8,128)S(1)} %broadcast_in_dim.85, s32[2]{0:T(128)S(1)} %fusion.50, f32[2,128,8,128]{3,2,1,0:T(8,128)S(1)} %copy.32), kind=kCustom, calls=%fused_computation | custom fusion | flops 262144 | bytes 3145736 | tf_op jit(solution)/shard_map/scatter-add | solution.py:95
  65.2 0.1 convert_element_type.35
  65.3 1.2 %reshape.158 = bf16[1,384,1024]{2,1,0:T(8,128)(2,1)} reshape(bf16[3,128,8,128]{3,2,1,0:T(8,128)(2,1)S(1)} %convert_element_type.35) | data formatting | bytes 1572864 | tf_op jit(solution)/shard_map/reshape | solution.py:97
  66.5 0.0 collective-permute-done.4
  66.5 0.0 collective-permute-done.5
  66.5 1.7 %fusion.43 = bf16[384,128]{1,0:T(8,128)(2,1)} fusion(f32[384,128]{1,0:T(8,128)} %collective-permute-done.5, f32[384,128]{1,0:T(8,128)} %collective-permute-done.4, f32[3,128,128]{2,1,0:T(8,128)S(1)} %copy.34), kind=kLoop, calls=%fused_computation.56 | loop fusion | flops 147456 | bytes 688128 | tf_op jit(solution)/shard_map/convert_element_type | solution.py:134
  68.2 1.4 %collective-permute-done.6 = f32[384,128]{1,0:T(8,128)} collective-permute-done((f32[384,128]{1,0:T(8,128)S(1)}, f32[384,128]{1,0:T(8,128)}, u32[]{:S(2)}, u32[]{:S(2)}) %collective-permute-start.6) | collective-permute-done | bytes 196640 | tf_op jit(solution)/shard_map/ppermute | solution.py:14
  69.6 1.6 %collective-permute-done.7 = f32[384,128]{1,0:T(8,128)} collective-permute-done((f32[384,128]{1,0:T(8,128)}, f32[384,128]{1,0:T(8,128)}, u32[]{:S(2)}, u32[]{:S(2)}) %collective-permute-start.7) | collective-permute-done | bytes 196640 | tf_op jit(solution)/shard_map/ppermute | solution.py:14
  71.2 1.7 %fusion.41 = bf16[384,128]{1,0:T(8,128)(2,1)} fusion(f32[384,128]{1,0:T(8,128)} %collective-permute-done.7, f32[384,128]{1,0:T(8,128)} %collective-permute-done.6, f32[3,128,128]{2,1,0:T(8,128)S(1)} %copy.37), kind=kLoop, calls=%fused_computation.53 | loop fusion | flops 147456 | bytes 688128 | tf_op jit(solution)/shard_map/convert_element_type | solution.py:135
  (24 shorter events, 0.3 us)
Async XLA Ops:
  0.6 18.8 %copy-start = (s32[1,48]{1,0:T(1,128)S(1)}, s32[1,48]{1,0:T(1,128)}, u32[]{:S(2)}) copy-start(s32[1,48]{1,0:T(1,128)} %param.13) | copy-start | bytes 580
  0.6 19.5 %copy-start.1 = (bf16[1,384,128]{2,1,0:T(8,128)(2,1)S(1)}, bf16[1,384,128]{2,1,0:T(8,128)(2,1)}, u32[]{:S(2)}) copy-start(bf16[1,384,128]{2,1,0:T(8,128)(2,1)} %param.9) | copy-start | bytes 294916
  0.7 19.6 %copy-start.2 = (bf16[1,384,128]{2,1,0:T(8,128)(2,1)S(1)}, bf16[1,384,128]{2,1,0:T(8,128)(2,1)}, u32[]{:S(2)}) copy-start(bf16[1,384,128]{2,1,0:T(8,128)(2,1)} %param.10) | copy-start | bytes 294916
  0.7 19.5 %collective-permute-start.1 = (bf16[384,128]{1,0:T(8,128)(2,1)}, bf16[384,128]{1,0:T(8,128)(2,1)S(1)}, u32[]{:S(2)}, u32[]{:S(2)}) collective-permute-start(bf16[384,128]{1,0:T(8,128)(2,1)} %bitcast.183), channel_id=1, source_target_pairs={{0,8},{8,16},{16,24},{24,32},{32,40},{40,48},{48,56},{56,64},{64,7... | collective-permute-start | bytes 294920 | tf_op jit(solution)/shard_map/ppermute | solution.py:14
  5.5 14.6 %collective-permute-start = (bf16[384,128]{1,0:T(8,128)(2,1)}, bf16[384,128]{1,0:T(8,128)(2,1)S(1)}, u32[]{:S(2)}, u32[]{:S(2)}) collective-permute-start(bf16[384,128]{1,0:T(8,128)(2,1)} %bitcast.184), channel_id=1, source_target_pairs={{0,16},{8,24},{16,32},{24,40},{32,48},{40,56},{48,64},{56,72},{64,... | collective-permute-start | bytes 294920 | tf_op jit(solution)/shard_map/ppermute | solution.py:14
  8.8 11.4 %collective-permute-start.3 = (bf16[384,128]{1,0:T(8,128)(2,1)}, bf16[384,128]{1,0:T(8,128)(2,1)S(1)}, u32[]{:S(2)}, u32[]{:S(2)}) collective-permute-start(bf16[384,128]{1,0:T(8,128)(2,1)} %bitcast.186), channel_id=1, source_target_pairs={{0,8},{8,16},{16,24},{24,32},{32,40},{40,48},{48,56},{56,64},{64,7... | collective-permute-start | bytes 294920 | tf_op jit(solution)/shard_map/ppermute | solution.py:14
  11.0 9.1 %collective-permute-start.2 = (bf16[384,128]{1,0:T(8,128)(2,1)}, bf16[384,128]{1,0:T(8,128)(2,1)S(1)}, u32[]{:S(2)}, u32[]{:S(2)}) collective-permute-start(bf16[384,128]{1,0:T(8,128)(2,1)} %bitcast.187), channel_id=1, source_target_pairs={{0,16},{8,24},{16,32},{24,40},{32,48},{40,56},{48,64},{56,72},{64,... | collective-permute-start | bytes 294920 | tf_op jit(solution)/shard_map/ppermute | solution.py:14
  49.0 17.5 %collective-permute-start.4 = (f32[384,128]{1,0:T(8,128)S(1)}, f32[384,128]{1,0:T(8,128)}, u32[]{:S(2)}, u32[]{:S(2)}) collective-permute-start(f32[384,128]{1,0:T(8,128)S(1)} %bitcast.181), channel_id=1, source_target_pairs={{8,0},{16,8},{24,16},{32,24},{40,32},{48,40},{56,48},{64,56},{72,6... | collective-permute-start | bytes 589832 | tf_op jit(solution)/shard_map/ppermute | solution.py:14
  57.4 9.2 %collective-permute-start.5 = (f32[384,128]{1,0:T(8,128)}, f32[384,128]{1,0:T(8,128)}, u32[]{:S(2)}, u32[]{:S(2)}) collective-permute-start(f32[384,128]{1,0:T(8,128)} %concatenate.14), channel_id=1, source_target_pairs={{16,0},{24,8},{32,16},{40,24},{48,32},{56,40},{64,48},{72,56},{80,... | collective-permute-start | bytes 589832 | tf_op jit(solution)/shard_map/ppermute | solution.py:14
  59.5 10.1 %collective-permute-start.6 = (f32[384,128]{1,0:T(8,128)S(1)}, f32[384,128]{1,0:T(8,128)}, u32[]{:S(2)}, u32[]{:S(2)}) collective-permute-start(f32[384,128]{1,0:T(8,128)S(1)} %bitcast.182), channel_id=1, source_target_pairs={{8,0},{16,8},{24,16},{32,24},{40,32},{48,40},{56,48},{64,56},{72,6... | collective-permute-start | bytes 589832 | tf_op jit(solution)/shard_map/ppermute | solution.py:14
  61.4 9.8 %collective-permute-start.7 = (f32[384,128]{1,0:T(8,128)}, f32[384,128]{1,0:T(8,128)}, u32[]{:S(2)}, u32[]{:S(2)}) collective-permute-start(f32[384,128]{1,0:T(8,128)} %concatenate.15), channel_id=1, source_target_pairs={{16,0},{24,8},{32,16},{40,24},{48,32},{56,40},{64,48},{72,56},{80,... | collective-permute-start | bytes 589832 | tf_op jit(solution)/shard_map/ppermute | solution.py:14
where the time goes:
time: 73.5 us; the launch traced here: 72.9 us
  starting transfers between devices  25.8 us (35%)
  local copies, waits for them, and re-layouts  14.8 us (20%)
  matrix products  12.3 us (17%)
  other arithmetic  8.23 us (11%)
  loops' own time  7.77 us (11%)
  waiting for transfers between devices  2.97 us (4%)
  between operations  0.92 us (1%)
    ppermute x8, starting transfers between devices, shifted(): return lax.ppermute(block, axis, route)  25.8 us
    another operation x1, loops' own time, per_device(): lax.map(slot_grads, (slot_block, slot_live))  7.77 us
    dynamic_slice x4, local copies, waits for them, and re-layouts, per_device(): lax.map(slot_grads, (slot_block, slot_live))  3.65 us
    ppermute x8, waiting for transfers between devices, shifted(): return lax.ppermute(block, axis, route)  2.97 us
    dot_general x2, matrix products, slot_grads(): jnp.einsum('bhd,kd->hbk', grad_block, value_window, preferred_element_typ...  2.82 us
    dynamic_slice x2, local copies, waits for them, and re-layouts, slot_grads(): lax.dynamic_index_in_dim(start_local, block_index, 0, keepdims=False) * BLK  2.66 us
    dot_general x2, matrix products, slot_grads(): jnp.einsum('hbk,bhd->kd', attention_low, grad_block, preferred_element_ty...  2.64 us
    unnamed x8, local copies, waits for them, and re-layouts  2.63 us
  transfers between devices with their start and end apart: 8, of which 2 were waited for; matrix products, arithmetic and copies ran while one was open for 17% of the time, Pallas kernels for 0%

commit v1 on v0

v1 whole, which is shorter than its diff:
```python
import math

import jax
import jax.numpy as jnp
from jax import lax
from jax.experimental import pallas as pl
from jax.experimental.pallas import tpu as pltpu
from jax.sharding import PartitionSpec as P

BLK = 128
QH = 8
NB = 3
REACH = 4
WIN = REACH + NB
SLOT = QH * BLK
UNIT = 2 * BLK
UNITS = SLOT // UNIT
MESH = pl.DeviceIdType.MESH
F32 = jnp.float32
BF16 = jnp.bfloat16


def dot_nt(a, b):
    return lax.dot_general(a, b, (((1,), (1,)), ((), ())), preferred_element_type=F32)


def dot_nn(a, b):
    return lax.dot_general(a, b, (((1,), (0,)), ((), ())), preferred_element_type=F32)


def sub_sum(x):
    return jnp.sum(x.reshape(x.shape[0] // 8, 8, x.shape[1]), axis=0)


def kernel(
    ranks,
    assist,
    first,
    q_hbm,
    k_hbm,
    v_hbm,
    g_hbm,
    dq_out,
    dk_out,
    dv_out,
    q_in,
    g_in,
    win_k,
    win_v,
    q_all,
    g_all,
    k_t,
    w_buf,
    d_buf,
    ds_buf,
    l_buf,
    e_buf,
    acc_k,
    acc_v,
    out_k,
    out_v,
    near_k,
    near_v,
    far_k,
    far_v,
    dq_slot,
    in_sem,
    fs_sem,
    fr_sem,
    bs_sem,
    br_sem,
):
    me = lax.axis_index("ctx")
    scale = 1.0 / math.sqrt(BLK)
    base = me * NB
    halo = REACH * BLK

    local = [
        pltpu.make_async_copy(k_hbm, win_k.at[pl.ds(halo, NB * BLK)], in_sem.at[0]),
        pltpu.make_async_copy(v_hbm, win_v.at[pl.ds(halo, NB * BLK)], in_sem.at[1]),
        pltpu.make_async_copy(q_hbm, q_in, in_sem.at[2]),
        pltpu.make_async_copy(g_hbm, g_in, in_sem.at[3]),
    ]
    for copy in local:
        copy.start()

    def halo_copy(array, block, window, away, slot):
        src = (k_hbm, v_hbm)[array].at[pl.ds(block * BLK, BLK)]
        dst = (win_k, win_v)[array].at[pl.ds(window * BLK, BLK)]
        return pltpu.make_async_remote_copy(
            src_ref=src,
            dst_ref=dst,
            send_sem=fs_sem.at[slot],
            recv_sem=fr_sem.at[slot],
            device_id={"ctx": me + away},
            device_id_type=MESH,
        )

    halo_copies = []
    for window in (0, 1, 2, 3):
        away = 2 if window == 0 else 1
        block = NB - 1 if window == 0 else window - 1
        for array in (0, 1):
            halo_copies.append(
                (away, window, halo_copy(array, block, window, away, 2 * window + array))
            )

    def back_copy(array, window, slot):
        src = (out_k, out_v)[array].at[pl.ds(window * BLK, BLK)]
        if window == 0:
            dst = (far_k, far_v)[array]
        else:
            dst = (near_k, near_v)[array].at[pl.ds((window - 1) * BLK, BLK)]
        away = 2 if window == 0 else 1
        return pltpu.make_async_remote_copy(
            src_ref=src,
            dst_ref=dst,
            send_sem=bs_sem.at[slot],
            recv_sem=br_sem.at[slot],
            device_id={"ctx": me - away},
            device_id_type=MESH,
        )

    back_copies = []
    for window in (0, 1, 2, 3):
        away = 2 if window == 0 else 1
        for array in (0, 1):
            back_copies.append((away, window, back_copy(array, window, 2 * window + array)))

    barrier = pltpu.get_barrier_semaphore()
    for away in (1, 2):

        @pl.when(me >= away)
        def _():
            pl.semaphore_signal(
                barrier, inc=1, device_id={"ctx": me - away}, device_id_type=MESH
            )

        @pl.when(me + away < ranks)
        def _():
            pl.semaphore_signal(
                barrier, inc=1, device_id={"ctx": me + away}, device_id_type=MESH
            )

    pl.semaphore_wait(barrier, jnp.minimum(me, 2) + jnp.minimum(ranks - 1 - me, 2))

    for away, window, copy in halo_copies:

        @pl.when(me + away < ranks)
        def _():
            copy.start()

    for away, window, _ in halo_copies[::2]:

        @pl.when(me < away)
        def _():
            zero = jnp.zeros((BLK, BLK), BF16)
            win_k[window * BLK : (window + 1) * BLK, :] = zero
            win_v[window * BLK : (window + 1) * BLK, :] = zero

    for away, window, _ in back_copies[::2]:

        @pl.when(me + away >= ranks)
        def _():
            zero = jnp.zeros((BLK, BLK), BF16)
            if window == 0:
                far_k[...] = zero
                far_v[...] = zero
            else:
                near_k[(window - 1) * BLK : window * BLK, :] = zero
                near_v[(window - 1) * BLK : window * BLK, :] = zero

    mark = [assist[0, base + i] for i in range(NB)]
    turn = [first[0, base + i] for i in range(NB)]
    head_is_first = mark[0] == 1
    tail_is_last = mark[2] == 1
    slot_block = (jnp.where(head_is_first, 0, 1), jnp.where(tail_is_last, 2, 1))
    slot_turn = (
        jnp.where(head_is_first, turn[0], turn[1]),
        jnp.where(tail_is_last, turn[2], turn[1]),
    )
    slot_live = (
        jnp.maximum(mark[0], mark[1]),
        jnp.maximum(mark[2], mark[0] * mark[1]),
    )

    def valid(slot, window):
        seen = (base - REACH + window >= slot_turn[slot]) & (slot_live[slot] == 1)
        return jnp.where(seen, jnp.float32(1.0), jnp.float32(0.0))

    l_buf[...] = jnp.zeros_like(l_buf)
    e_buf[...] = jnp.zeros_like(e_buf)
    acc_k[...] = jnp.zeros_like(acc_k)
    acc_v[...] = jnp.zeros_like(acc_v)
    for copy in local:
        copy.wait()

    for slot in (0, 1):
        low = slice(slot * BLK, (slot + 1) * BLK)
        high = slice((slot + 1) * BLK, (slot + 2) * BLK)
        for head in range(QH):
            at = slot * SLOT + head * BLK
            cols = slice(head * BLK, (head + 1) * BLK)
            is_low = slot_block[slot] == slot
            q_all[at : at + BLK, :] = jnp.where(is_low, q_in[low, cols], q_in[high, cols])
            g_all[at : at + BLK, :] = jnp.where(is_low, g_in[low, cols], g_in[high, cols])

    ahead = (lax.broadcasted_iota(jnp.int32, (BLK, UNIT), 1) % BLK) - lax.broadcasted_iota(
        jnp.int32, (BLK, UNIT), 0
    )

    def weigh(slot, windows):
        def step(u, carry):
            unit = slot * UNITS + u
            at = pl.ds(pl.multiple_of(unit * UNIT, UNIT), UNIT)
            q_t = q_all[at, :]
            g_t = g_all[at, :]
            total = l_buf[unit]
            total_e = e_buf[unit]
            for window in windows:
                keys = slice(window * BLK, (window + 1) * BLK)
                scores = dot_nt(win_k[keys, :], q_t)
                prob_grad = dot_nt(win_v[keys, :], g_t)
                w = jnp.exp2(scores * (scale * math.log2(math.e)))
                if window >= REACH:
                    w = jnp.where(ahead >= (window - REACH - slot_block[slot]) * BLK, w, 0.0)
                w_buf[unit, keys, :] = w
                d_buf[unit, keys, :] = prob_grad
                on = valid(slot, window)
                total = total + on * sub_sum(w)
                total_e = total_e + on * sub_sum(w * prob_grad)
            l_buf[unit] = total
            e_buf[unit] = total_e
            return carry

        lax.fori_loop(0, UNITS, step, 0)

    own = ((4, 5), (4, 5, 6))
    other = ((0, 1, 2, 3), (1, 2, 3))
    for slot in (0, 1):
        weigh(slot, own[slot])

    for away, window, copy in halo_copies:

        @pl.when(me >= away)
        def _():
            copy.wait_recv()

    for slot in (0, 1):
        weigh(slot, other[slot])

    def finish(unit):
        total = jnp.sum(l_buf[unit], axis=0, keepdims=True)
        total_e = jnp.sum(e_buf[unit], axis=0, keepdims=True)
        inverse = jnp.where(total > 0.0, 1.0 / total, 0.0)
        return inverse, total_e * inverse

    def grads(slot, unit, windows):
        at = pl.ds(pl.multiple_of(unit * UNIT, UNIT), UNIT)
        q_t = q_all[at, :]
        g_t = g_all[at, :]
        inverse, delta = finish(unit)
        for window in windows:
            keys = slice(window * BLK, (window + 1) * BLK)
            attention = w_buf[unit, keys, :] * (inverse * valid(slot, window))
            score_grad = (attention * (d_buf[unit, keys, :] - delta)).astype(BF16)
            ds_buf[unit, keys, :] = score_grad
            acc_k[keys, :] += dot_nn(score_grad, q_t)
            acc_v[keys, :] += dot_nn(attention.astype(BF16), g_t)

    for slot in (0, 1):

        def far_step(u, carry):
            grads(slot, slot * UNITS + u, other[slot])
            return carry

        lax.fori_loop(0, UNITS, far_step, 0)

    out_k[...] = (acc_k[:halo, :] * scale).astype(BF16)
    out_v[...] = acc_v[:halo, :].astype(BF16)
    for away, window, copy in back_copies:

        @pl.when(me >= away)
        def _():
            copy.start()

    for window in range(WIN):
        keys = slice(window * BLK, (window + 1) * BLK)
        k_t[:, keys] = win_k[keys, :].T

    for slot in (0, 1):

        def own_step(u, carry):
            unit = slot * UNITS + u
            grads(slot, unit, own[slot])
            keys = slice(slot * BLK, (slot + WIN - 1) * BLK)
            part = dot_nn(k_t[:, keys], ds_buf[unit, keys, :]) * scale
            both = jnp.concatenate([part[:, :BLK].T, part[:, BLK:].T], axis=1)
            cols = pl.ds(pl.multiple_of(u * UNIT, UNIT), UNIT)
            dq_slot[slot, :, cols] = both.astype(BF16)
            return carry

        lax.fori_loop(0, UNITS, own_step, 0)

    for block in range(NB):
        rows = slice(block * BLK, (block + 1) * BLK)
        use = [(slot_block[s] == block) & (slot_live[s] == 1) for s in (0, 1)]
        value = jnp.where(use[1], dq_slot[1], jnp.zeros((), BF16))
        dq_out[rows, :] = jnp.where(use[0], dq_slot[0], value)

    for away, window, copy in back_copies:

        @pl.when(me + away < ranks)
        def _():
            copy.wait_recv()

    total_k = acc_k[halo:, :] * scale + near_k[...].astype(F32)
    total_v = acc_v[halo:, :] + near_v[...].astype(F32)
    last = (NB - 1) * BLK
    dk_out[:last, :] = total_k[:last].astype(BF16)
    dv_out[:last, :] = total_v[:last].astype(BF16)
    dk_out[last:, :] = (total_k[last:] + far_k[...].astype(F32)).astype(BF16)
    dv_out[last:, :] = (total_v[last:] + far_v[...].astype(F32)).astype(BF16)

    for away, window, copy in halo_copies:

        @pl.when(me + away < ranks)
        def _():
            copy.wait_send()

    for away, window, copy in back_copies:

        @pl.when(me >= away)
        def _():
            copy.wait_send()


def per_device(ranks, query_rows, key_rows, value_rows, out_grad, assistant, turn_first):
    rows = NB * BLK
    hbm = pl.BlockSpec(memory_space=pltpu.HBM)
    smem = pl.BlockSpec(memory_space=pltpu.SMEM)
    vmem = pl.BlockSpec(memory_space=pltpu.VMEM)
    units = 2 * UNITS
    scratch = [
        pltpu.VMEM((rows, SLOT), BF16),
        pltpu.VMEM((rows, SLOT), BF16),
        pltpu.VMEM((WIN * BLK, BLK), BF16),
        pltpu.VMEM((WIN * BLK, BLK), BF16),
        pltpu.VMEM((2 * SLOT, BLK), BF16),
        pltpu.VMEM((2 * SLOT, BLK), BF16),
        pltpu.VMEM((BLK, WIN * BLK), BF16),
        pltpu.VMEM((units, WIN * BLK, UNIT), F32),
        pltpu.VMEM((units, WIN * BLK, UNIT), F32),
        pltpu.VMEM((units, WIN * BLK, UNIT), BF16),
        pltpu.VMEM((units, 8, UNIT), F32),
        pltpu.VMEM((units, 8, UNIT), F32),
        pltpu.VMEM((WIN * BLK, BLK), F32),
        pltpu.VMEM((WIN * BLK, BLK), F32),
        pltpu.VMEM((REACH * BLK, BLK), BF16),
        pltpu.VMEM((REACH * BLK, BLK), BF16),
        pltpu.VMEM((rows, BLK), BF16),
        pltpu.VMEM((rows, BLK), BF16),
        pltpu.VMEM((BLK, BLK), BF16),
        pltpu.VMEM((BLK, BLK), BF16),
        pltpu.VMEM((2, BLK, SLOT), BF16),
        pltpu.SemaphoreType.DMA((4,)),
        pltpu.SemaphoreType.DMA((8,)),
        pltpu.SemaphoreType.DMA((8,)),
        pltpu.SemaphoreType.DMA((8,)),
        pltpu.SemaphoreType.DMA((8,)),
    ]

    blocks = [
        pltpu.with_memory_space_constraint(x[0], pltpu.HBM)
        for x in (query_rows, key_rows, value_rows, out_grad)
    ]

    def body(*refs):
        kernel(ranks, *refs)

    dq, dk, dv = pl.pallas_call(
        body,
        out_shape=(
            jax.ShapeDtypeStruct((rows, SLOT), BF16),
            jax.ShapeDtypeStruct((rows, BLK), BF16),
            jax.ShapeDtypeStruct((rows, BLK), BF16),
        ),
        in_specs=[smem, smem, hbm, hbm, hbm, hbm],
        out_specs=(vmem, vmem, vmem),
        scratch_shapes=scratch,
        compiler_params=pltpu.CompilerParams(
            collective_id=0, has_side_effects=True, vmem_limit_bytes=40 * 1024 * 1024
        ),
        name="attention_backward",
    )(assistant, turn_first, *blocks)
    return dq[None], dk[None], dv[None]


def solution(mesh):
    ranks = mesh.shape["ctx"]

    def step(*arrays):
        return per_device(ranks, *arrays)

    wide = P("dp", "ctx", "tp")
    return jax.shard_map(
        step,
        mesh=mesh,
        in_specs=(wide, wide, wide, wide, P("dp", None), P("dp", None)),
        out_specs=(wide, wide, wide),
        check_vma=False,
    )
```

time: 73.5 us -> 34.9 us (0.47)
  Pallas kernels: 0 us -> 31.2 us
  starting transfers between devices: 25.8 us -> 0 us
  matrix products: 12.3 us -> 0 us
  local copies, waits for them, and re-layouts: 14.8 us -> 2.82 us
  other arithmetic: 8.23 us -> 0 us
  loops' own time: 7.77 us -> 0 us
  waiting for transfers between devices: 2.97 us -> 0 us
    pallas_call x0 -> x1, Pallas kernels: none -> 31.2 us  [per_device(): pl.pallas_call(body, out_shape=(jax.ShapeDtypeStruct((rows, SLOT), BF16),...]
    ppermute x8 -> x0, starting transfers between devices: 25.8 us -> none  [shifted(): return lax.ppermute(block, axis, route)]
    dot_general x12 -> x0, matrix products: 12.3 us -> none  [the longest x2 2.82 us: slot_grads(): jnp.einsum('bhd,kd->hbk', grad_block, value_window, preferred_element_typ...]
    another operation x1 -> x0, loops' own time: 7.77 us -> none  [per_device(): lax.map(slot_grads, (slot_block, slot_live))]
    dynamic_slice x9 -> x0, local copies, waits for them, and re-layouts: 7.07 us -> none  [the longest x4 3.65 us: per_device(): lax.map(slot_grads, (slot_block, slot_live))]
    convert_element_type x5 -> x0, other arithmetic: 4.92 us -> none  [the longest x1 1.69 us: per_device(): key_grad = key_total.astype(jnp.bfloat16)]
    ppermute x8 -> x0, waiting for transfers between devices: 2.97 us -> none  [shifted(): return lax.ppermute(block, axis, route)]
    concatenate x2 -> x0, local copies, waits for them, and re-layouts: 1.37 us -> none  [the longest x1 0.69 us: per_device(): jnp.concatenate([filler, far_key_grad], 0)]
  transfers between devices with their start and end apart: 8 -> 0, of which waited for: 2 -> 0; matrix products, arithmetic and copies ran while one was open for 17% -> 0% of each run, Pallas kernels for 0% -> 0%
where the time goes in v1:
time: 34.9 us; the launch traced here: 34.7 us
  Pallas kernels  31.2 us (89%)
  local copies, waits for them, and re-layouts  2.82 us (8%)
  between operations  0.66 us (2%)
    pallas_call x1, Pallas kernels, per_device(): pl.pallas_call(body, out_shape=(jax.ShapeDtypeStruct((rows, SLOT), BF16),...  31.2 us
    unnamed x7, local copies, waits for them, and re-layouts  2.82 us

profile of v1, /device:TPU:1, one launch (start us, length us, event | category | flops | bytes accessed | tf_op | source)
XLA Modules:
  0.0 34.7 jit_solution(1886209224364080633)
XLA Ops:
  0.6 0.0 copy-start
  0.6 0.0 copy-start.1
  0.7 0.6 %copy-done = s32[1,48]{1,0:T(1,128)S(1)} copy-done((s32[1,48]{1,0:T(1,128)S(1)}, s32[1,48]{1,0:T(1,128)}, u32[]{:S(2)}) %copy-start) | copy-done | bytes 216
  1.3 0.0 copy-done.1
  1.3 31.2 %attention_backward.1 = (bf16[384,1024]{1,0:T(8,128)(2,1)S(1)}, bf16[384,128]{1,0:T(8,128)(2,1)S(1)}, bf16[384,128]{1,0:T(8,128)(2,1)S(1)}) custom-call(s32[1,48]{1,0:T(1,128)S(1)} %copy-done, s32[1,48]{1,0:T(1,128)S(1)} %copy-done.1, bf16[384,1024]{1,0:T(8,128)(2,1)} %bitcast.10, bf16[384,128]{1,0:T(8,128)(2,1)} %bitcast.12, bf16[384,128]{1,0:T(8,128)(2,1)} %bitcast.13, ...), custom_call_target="tpu_custom_call" | custom-call | tf_op jit(solution)/shard_map/attention_backward/pallas_call | solution.py:381
  32.5 0.9 %copy.12 = bf16[1,384,1024]{2,1,0:T(8,128)(2,1)} copy(bf16[1,384,1024]{2,1,0:T(8,128)(2,1)S(1)} %bitcast.7) | data formatting | bytes 1572864
  33.4 0.6 %copy.13 = bf16[1,384,128]{2,1,0:T(8,128)(2,1)} copy(bf16[1,384,128]{2,1,0:T(8,128)(2,1)S(1)} %bitcast.9) | data formatting | bytes 196608
  34.0 0.6 %copy.14 = bf16[1,384,128]{2,1,0:T(8,128)(2,1)} copy(bf16[1,384,128]{2,1,0:T(8,128)(2,1)S(1)} %bitcast.8) | data formatting | bytes 196608
Async XLA Ops:
  0.6 0.7 %copy-start = (s32[1,48]{1,0:T(1,128)S(1)}, s32[1,48]{1,0:T(1,128)}, u32[]{:S(2)}) copy-start(s32[1,48]{1,0:T(1,128)} %refs_0_.1) | copy-start | bytes 580
  0.6 0.7 %copy-start.1 = (s32[1,48]{1,0:T(1,128)S(1)}, s32[1,48]{1,0:T(1,128)}, u32[]{:S(2)}) copy-start(s32[1,48]{1,0:T(1,128)} %refs_1_.1) | copy-start | bytes 580

commit v2 on v1

--- a/solution.py
+++ b/solution.py
@@ -34,8 +34,8 @@
 
 def kernel(
     ranks,
-    assist,
-    first,
+    assist_hbm,
+    first_hbm,
     q_hbm,
     k_hbm,
     v_hbm,
@@ -64,6 +64,8 @@
     far_k,
     far_v,
     dq_slot,
+    assist,
+    first,
     in_sem,
     fs_sem,
     fr_sem,
@@ -80,6 +82,8 @@
         pltpu.make_async_copy(v_hbm, win_v.at[pl.ds(halo, NB * BLK)], in_sem.at[1]),
         pltpu.make_async_copy(q_hbm, q_in, in_sem.at[2]),
         pltpu.make_async_copy(g_hbm, g_in, in_sem.at[3]),
+        pltpu.make_async_copy(assist_hbm, assist, in_sem.at[4]),
+        pltpu.make_async_copy(first_hbm, first, in_sem.at[5]),
     ]
     for copy in local:
         copy.start()
@@ -170,6 +174,9 @@
                 near_k[(window - 1) * BLK : window * BLK, :] = zero
                 near_v[(window - 1) * BLK : window * BLK, :] = zero
 
+    for copy in local:
+        copy.wait()
+
     mark = [assist[0, base + i] for i in range(NB)]
     turn = [first[0, base + i] for i in range(NB)]
     head_is_first = mark[0] == 1
@@ -188,13 +195,6 @@
         seen = (base - REACH + window >= slot_turn[slot]) & (slot_live[slot] == 1)
         return jnp.where(seen, jnp.float32(1.0), jnp.float32(0.0))
 
-    l_buf[...] = jnp.zeros_like(l_buf)
-    e_buf[...] = jnp.zeros_like(e_buf)
-    acc_k[...] = jnp.zeros_like(acc_k)
-    acc_v[...] = jnp.zeros_like(acc_v)
-    for copy in local:
-        copy.wait()
-
     for slot in (0, 1):
         low = slice(slot * BLK, (slot + 1) * BLK)
         high = slice((slot + 1) * BLK, (slot + 2) * BLK)
@@ -209,14 +209,13 @@
         jnp.int32, (BLK, UNIT), 0
     )
 
-    def weigh(slot, windows):
-        def step(u, carry):
-            unit = slot * UNITS + u
-            at = pl.ds(pl.multiple_of(unit * UNIT, UNIT), UNIT)
+    def weigh(slot, windows, opens):
+        for unit in range(slot * UNITS, (slot + 1) * UNITS):
+            at = slice(unit * UNIT, (unit + 1) * UNIT)
             q_t = q_all[at, :]
             g_t = g_all[at, :]
-            total = l_buf[unit]
-            total_e = e_buf[unit]
+            total = None if opens else l_buf[unit]
+            total_e = None if opens else e_buf[unit]
             for window in windows:
                 keys = slice(window * BLK, (window + 1) * BLK)
                 scores = dot_nt(win_k[keys, :], q_t)
@@ -227,27 +226,12 @@
                 w_buf[unit, keys, :] = w
                 d_buf[unit, keys, :] = prob_grad
                 on = valid(slot, window)
-                total = total + on * sub_sum(w)
-                total_e = total_e + on * sub_sum(w * prob_grad)
+                more = on * sub_sum(w)
+                more_e = on * sub_sum(w * prob_grad)
+                total = more if total is None else total + more
+                total_e = more_e if total_e is None else total_e + more_e
             l_buf[unit] = total
             e_buf[unit] = total_e
-            return carry
-
-        lax.fori_loop(0, UNITS, step, 0)
-
-    own = ((4, 5), (4, 5, 6))
-    other = ((0, 1, 2, 3), (1, 2, 3))
-    for slot in (0, 1):
-        weigh(slot, own[slot])
-
-    for away, window, copy in halo_copies:
-
-        @pl.when(me >= away)
-        def _():
-            copy.wait_recv()
-
-    for slot in (0, 1):
-        weigh(slot, other[slot])
 
     def finish(unit):
         total = jnp.sum(l_buf[unit], axis=0, keepdims=True)
@@ -255,52 +239,71 @@
         inverse = jnp.where(total > 0.0, 1.0 / total, 0.0)
         return inverse, total_e * inverse
 
-    def grads(slot, unit, windows):
-        at = pl.ds(pl.multiple_of(unit * UNIT, UNIT), UNIT)
-        q_t = q_all[at, :]
-        g_t = g_all[at, :]
-        inverse, delta = finish(unit)
+    written = set()
+
+    def grads(slot, windows):
+        for unit in range(slot * UNITS, (slot + 1) * UNITS):
+            at = slice(unit * UNIT, (unit + 1) * UNIT)
+            q_t = q_all[at, :]
+            g_t = g_all[at, :]
+            inverse, delta = finish(unit)
+            for window in windows:
+                keys = slice(window * BLK, (window + 1) * BLK)
+                attention = w_buf[unit, keys, :] * (inverse * valid(slot, window))
+                score_grad = (attention * (d_buf[unit, keys, :] - delta)).astype(BF16)
+                ds_buf[unit, keys, :] = score_grad
+                part_k = dot_nn(score_grad, q_t)
+                part_v = dot_nn(attention.astype(BF16), g_t)
+                if window in written:
+                    part_k = acc_k[keys, :] + part_k
+                    part_v = acc_v[keys, :] + part_v
+                written.add(window)
+                acc_k[keys, :] = part_k
+                acc_v[keys, :] = part_v
+
+    def received(copies, windows):
+        for away, window, copy in copies:
+            if window in windows:
+
+                @pl.when(me >= away)
+                def _():
+                    copy.wait_recv()
+
+    def give_back(windows):
         for window in windows:
             keys = slice(window * BLK, (window + 1) * BLK)
-            attention = w_buf[unit, keys, :] * (inverse * valid(slot, window))
-            score_grad = (attention * (d_buf[unit, keys, :] - delta)).astype(BF16)
-            ds_buf[unit, keys, :] = score_grad
-            acc_k[keys, :] += dot_nn(score_grad, q_t)
-            acc_v[keys, :] += dot_nn(attention.astype(BF16), g_t)
-
-    for slot in (0, 1):
-
-        def far_step(u, carry):
-            grads(slot, slot * UNITS + u, other[slot])
-            return carry
-
-        lax.fori_loop(0, UNITS, far_step, 0)
-
-    out_k[...] = (acc_k[:halo, :] * scale).astype(BF16)
-    out_v[...] = acc_v[:halo, :].astype(BF16)
-    for away, window, copy in back_copies:
-
-        @pl.when(me >= away)
-        def _():
-            copy.start()
+            out_k[keys, :] = (acc_k[keys, :] * scale).astype(BF16)
+            out_v[keys, :] = acc_v[keys, :].astype(BF16)
+        for away, window, copy in back_copies:
+            if window in windows:
+
+                @pl.when(me >= away)
+                def _():
+                    copy.start()
+
+    weigh(0, (4, 5), True)
+    weigh(1, (4, 5, 6), True)
+    received(halo_copies, (1, 2, 3))
+    weigh(1, (1, 2, 3), False)
+    weigh(0, (1, 2, 3), False)
+    grads(1, (1, 2, 3))
+    received(halo_copies, (0,))
+    weigh(0, (0,), False)
+    grads(0, (1, 2, 3))
+    give_back((1, 2, 3))
+    grads(0, (0,))
+    give_back((0,))
 
     for window in range(WIN):
         keys = slice(window * BLK, (window + 1) * BLK)
         k_t[:, keys] = win_k[keys, :].T
-
-    for slot in (0, 1):
-
-        def own_step(u, carry):
-            unit = slot * UNITS + u
-            grads(slot, unit, own[slot])
-            keys = slice(slot * BLK, (slot + WIN - 1) * BLK)
-            part = dot_nn(k_t[:, keys], ds_buf[unit, keys, :]) * scale
+    for slot, windows in ((0, (4, 5)), (1, (4, 5, 6))):
+        grads(slot, windows)
+        keys = slice(slot * BLK, (slot + WIN - 1) * BLK)
+        for u in range(UNITS):
+            part = dot_nn(k_t[:, keys], ds_buf[slot * UNITS + u, keys, :]) * scale
             both = jnp.concatenate([part[:, :BLK].T, part[:, BLK:].T], axis=1)
-            cols = pl.ds(pl.multiple_of(u * UNIT, UNIT), UNIT)
-            dq_slot[slot, :, cols] = both.astype(BF16)
-            return carry
-
-        lax.fori_loop(0, UNITS, own_step, 0)
+            dq_slot[slot, :, u * UNIT : (u + 1) * UNIT] = both.astype(BF16)
 
     for block in range(NB):
         rows = slice(block * BLK, (block + 1) * BLK)
@@ -335,10 +338,21 @@
             copy.wait_send()
 
 
+def put_out(dq_in, dk_in, dv_in, dq_hbm, dk_hbm, dv_hbm, sem):
+    copies = [
+        pltpu.make_async_copy(dq_in, dq_hbm, sem.at[0]),
+        pltpu.make_async_copy(dk_in, dk_hbm, sem.at[1]),
+        pltpu.make_async_copy(dv_in, dv_hbm, sem.at[2]),
+    ]
+    for copy in copies:
+        copy.start()
+    for copy in copies:
+        copy.wait()
+
+
 def per_device(ranks, query_rows, key_rows, value_rows, out_grad, assistant, turn_first):
     rows = NB * BLK
     hbm = pl.BlockSpec(memory_space=pltpu.HBM)
-    smem = pl.BlockSpec(memory_space=pltpu.SMEM)
     vmem = pl.BlockSpec(memory_space=pltpu.VMEM)
     units = 2 * UNITS
     scratch = [
@@ -363,7 +377,9 @@
         pltpu.VMEM((BLK, BLK), BF16),
         pltpu.VMEM((BLK, BLK), BF16),
         pltpu.VMEM((2, BLK, SLOT), BF16),
-        pltpu.SemaphoreType.DMA((4,)),
+        pltpu.SMEM((1, assistant.shape[1]), jnp.int32),
+        pltpu.SMEM((1, assistant.shape[1]), jnp.int32),
+        pltpu.SemaphoreType.DMA((6,)),
         pltpu.SemaphoreType.DMA((8,)),
         pltpu.SemaphoreType.DMA((8,)),
         pltpu.SemaphoreType.DMA((8,)),
@@ -371,28 +387,38 @@
     ]
 
     blocks = [
-        pltpu.with_memory_space_constraint(x[0], pltpu.HBM)
-        for x in (query_rows, key_rows, value_rows, out_grad)
+        pltpu.with_memory_space_constraint(x, pltpu.HBM)
+        for x in (assistant, turn_first, query_rows[0], key_rows[0], value_rows[0], out_grad[0])
     ]
 
     def body(*refs):
         kernel(ranks, *refs)
 
-    dq, dk, dv = pl.pallas_call(
+    shapes = (
+        jax.ShapeDtypeStruct((rows, SLOT), BF16),
+        jax.ShapeDtypeStruct((rows, BLK), BF16),
+        jax.ShapeDtypeStruct((rows, BLK), BF16),
+    )
+    held = pl.pallas_call(
         body,
-        out_shape=(
-            jax.ShapeDtypeStruct((rows, SLOT), BF16),
-            jax.ShapeDtypeStruct((rows, BLK), BF16),
-            jax.ShapeDtypeStruct((rows, BLK), BF16),
-        ),
-        in_specs=[smem, smem, hbm, hbm, hbm, hbm],
+        out_shape=shapes,
+        in_specs=[hbm, hbm, hbm, hbm, hbm, hbm],
         out_specs=(vmem, vmem, vmem),
         scratch_shapes=scratch,
         compiler_params=pltpu.CompilerParams(
             collective_id=0, has_side_effects=True, vmem_limit_bytes=40 * 1024 * 1024
         ),
         name="attention_backward",
-    )(assistant, turn_first, *blocks)
+    )(*blocks)
+    dq, dk, dv = pl.pallas_call(
+        put_out,
+        out_shape=shapes,
+        in_specs=[vmem, vmem, vmem],
+        out_specs=(hbm, hbm, hbm),
+        scratch_shapes=[pltpu.SemaphoreType.DMA((3,))],
+        compiler_params=pltpu.CompilerParams(vmem_limit_bytes=4 * 1024 * 1024),
+        name="put_out",
+    )(*held)
     return dq[None], dk[None], dv[None]
 
 

time: 34.9 us -> 29.4 us (0.84)
  local copies, waits for them, and re-layouts: 2.82 us -> 0 us
  Pallas kernels: 31.2 us -> 28.6 us
    unnamed x7 -> x0, local copies, waits for them, and re-layouts: 2.82 us -> none
    pallas_call x1 -> x2, Pallas kernels: 31.2 us -> 28.6 us  [the longest x1 27.6 us: per_device(): pl.pallas_call(body, out_shape=shapes, in_specs=[hbm, hbm, hbm, hbm, hbm,...]
where the time goes in v2:
time: 29.4 us; the launch traced here: 29.2 us
  Pallas kernels  28.6 us (97%)
  between operations  0.64 us (2%)
    pallas_call x1, Pallas kernels, per_device(): pl.pallas_call(body, out_shape=shapes, in_specs=[hbm, hbm, hbm, hbm, hbm,...  27.6 us
    pallas_call x1, Pallas kernels, per_device(): pl.pallas_call(put_out, out_shape=shapes, in_specs=[vmem, vmem, vmem], ou...  0.96 us

profile of v2, /device:TPU:1, one launch (start us, length us, event | category | flops | bytes accessed | tf_op | source)
XLA Modules:
  0.0 29.2 jit_solution(767597189194376076)
XLA Ops:
  0.6 27.6 %attention_backward.1 = (bf16[384,1024]{1,0:T(8,128)(2,1)S(1)}, bf16[384,128]{1,0:T(8,128)(2,1)S(1)}, bf16[384,128]{1,0:T(8,128)(2,1)S(1)}) custom-call(s32[1,48]{1,0:T(1,128)} %refs_0_.1, s32[1,48]{1,0:T(1,128)} %refs_1_.1, bf16[384,1024]{1,0:T(8,128)(2,1)} %bitcast.7, bf16[384,128]{1,0:T(8,128)(2,1)} %bitcast.9, bf16[384,128]{1,0:T(8,128)(2,1)} %bitcast.10, ...), custom_call_target="tpu_custom_call" | custom-call | tf_op jit(solution)/shard_map/attention_backward/pallas_call | solution.py:402
  28.3 1.0 %put_out.1 = (bf16[384,1024]{1,0:T(8,128)(2,1)}, bf16[384,128]{1,0:T(8,128)(2,1)}, bf16[384,128]{1,0:T(8,128)(2,1)}) custom-call(bf16[384,1024]{1,0:T(8,128)(2,1)S(1)} %get-tuple-element.9.dq_in, bf16[384,128]{1,0:T(8,128)(2,1)S(1)} %get-tuple-element.10.dk_in, bf16[384,128]{1,0:T(8,128)(2,1)S(1)} %get-tuple-element.11.dv_in), custom_call_target="tpu_custom_call" | custom-call | tf_op jit(solution)/shard_map/put_out/pallas_call | solution.py:413

commit v3 on v2

--- a/solution.py
+++ b/solution.py
@@ -63,7 +63,6 @@
     near_v,
     far_k,
     far_v,
-    dq_slot,
     assist,
     first,
     in_sem,
@@ -140,13 +139,9 @@
                 barrier, inc=1, device_id={"ctx": me - away}, device_id_type=MESH
             )
 
-        @pl.when(me + away < ranks)
-        def _():
-            pl.semaphore_signal(
-                barrier, inc=1, device_id={"ctx": me + away}, device_id_type=MESH
-            )
-
-    pl.semaphore_wait(barrier, jnp.minimum(me, 2) + jnp.minimum(ranks - 1 - me, 2))
+    @pl.when(me < ranks - 1)
+    def _():
+        pl.semaphore_wait(barrier, jnp.minimum(ranks - 1 - me, 2))
 
     for away, window, copy in halo_copies:
 
@@ -233,7 +228,14 @@
             l_buf[unit] = total
             e_buf[unit] = total_e
 
+    finished = {}
+
     def finish(unit):
+        if unit not in finished:
+            finished[unit] = normalise(unit)
+        return finished[unit]
+
+    def normalise(unit):
         total = jnp.sum(l_buf[unit], axis=0, keepdims=True)
         total_e = jnp.sum(e_buf[unit], axis=0, keepdims=True)
         inverse = jnp.where(total > 0.0, 1.0 / total, 0.0)
@@ -289,27 +291,30 @@
     grads(1, (1, 2, 3))
     received(halo_copies, (0,))
     weigh(0, (0,), False)
-    grads(0, (1, 2, 3))
-    give_back((1, 2, 3))
-    grads(0, (0,))
-    give_back((0,))
+    for windows in ((1,), (2,), (3,), (0,)):
+        grads(0, windows)
+        give_back(windows)
 
     for window in range(WIN):
         keys = slice(window * BLK, (window + 1) * BLK)
         k_t[:, keys] = win_k[keys, :].T
+    zero = jnp.zeros((), BF16)
     for slot, windows in ((0, (4, 5)), (1, (4, 5, 6))):
         grads(slot, windows)
         keys = slice(slot * BLK, (slot + WIN - 1) * BLK)
         for u in range(UNITS):
             part = dot_nn(k_t[:, keys], ds_buf[slot * UNITS + u, keys, :]) * scale
-            both = jnp.concatenate([part[:, :BLK].T, part[:, BLK:].T], axis=1)
-            dq_slot[slot, :, u * UNIT : (u + 1) * UNIT] = both.astype(BF16)
-
-    for block in range(NB):
-        rows = slice(block * BLK, (block + 1) * BLK)
-        use = [(slot_block[s] == block) & (slot_live[s] == 1) for s in (0, 1)]
-        value = jnp.where(use[1], dq_slot[1], jnp.zeros((), BF16))
-        dq_out[rows, :] = jnp.where(use[0], dq_slot[0], value)
+            both = jnp.concatenate([part[:, :BLK].T, part[:, BLK:].T], axis=1).astype(BF16)
+            cols = slice(u * UNIT, (u + 1) * UNIT)
+            is_low = slot_block[slot] == slot
+            if slot == 0:
+                dq_out[:BLK, cols] = jnp.where(is_low, both, zero)
+                dq_out[BLK : 2 * BLK, cols] = jnp.where(is_low, zero, both)
+            else:
+                middle = dq_out[BLK : 2 * BLK, cols]
+                take = is_low & (slot_live[1] == 1)
+                dq_out[BLK : 2 * BLK, cols] = jnp.where(take, both, middle)
+                dq_out[2 * BLK :, cols] = jnp.where(is_low, zero, both)
 
     for away, window, copy in back_copies:
 
@@ -376,7 +381,6 @@
         pltpu.VMEM((rows, BLK), BF16),
         pltpu.VMEM((BLK, BLK), BF16),
         pltpu.VMEM((BLK, BLK), BF16),
-        pltpu.VMEM((2, BLK, SLOT), BF16),
         pltpu.SMEM((1, assistant.shape[1]), jnp.int32),
         pltpu.SMEM((1, assistant.shape[1]), jnp.int32),
         pltpu.SemaphoreType.DMA((6,)),

time: 29.4 us -> 25 us (0.85)
  Pallas kernels: 28.6 us -> 24.2 us
    pallas_call x1, Pallas kernels: 27.6 us -> 23.3 us  [per_device(): pl.pallas_call(body, out_shape=shapes, in_specs=[hbm, hbm, hbm, hbm, hbm,...]
where the time goes in v3:
time: 25 us; the launch traced here: 24.9 us
  Pallas kernels  24.2 us (97%)
  between operations  0.64 us (3%)
    pallas_call x1, Pallas kernels, per_device(): pl.pallas_call(body, out_shape=shapes, in_specs=[hbm, hbm, hbm, hbm, hbm,...  23.3 us
    pallas_call x1, Pallas kernels, per_device(): pl.pallas_call(put_out, out_shape=shapes, in_specs=[vmem, vmem, vmem], ou...  0.96 us

profile of v3, /device:TPU:1, one launch (start us, length us, event | category | flops | bytes accessed | tf_op | source)
XLA Modules:
  0.0 24.9 jit_solution(7070340298272002006)
XLA Ops:
  0.6 23.3 %attention_backward.1 = (bf16[384,1024]{1,0:T(8,128)(2,1)S(1)}, bf16[384,128]{1,0:T(8,128)(2,1)S(1)}, bf16[384,128]{1,0:T(8,128)(2,1)S(1)}) custom-call(s32[1,48]{1,0:T(1,128)} %refs_0_.1, s32[1,48]{1,0:T(1,128)} %refs_1_.1, bf16[384,1024]{1,0:T(8,128)(2,1)} %bitcast.7, bf16[384,128]{1,0:T(8,128)(2,1)} %bitcast.9, bf16[384,128]{1,0:T(8,128)(2,1)} %bitcast.10, ...), custom_call_target="tpu_custom_call" | custom-call | tf_op jit(solution)/shard_map/attention_backward/pallas_call | solution.py:406
  23.9 1.0 %put_out.1 = (bf16[384,1024]{1,0:T(8,128)(2,1)}, bf16[384,128]{1,0:T(8,128)(2,1)}, bf16[384,128]{1,0:T(8,128)(2,1)}) custom-call(bf16[384,1024]{1,0:T(8,128)(2,1)S(1)} %get-tuple-element.9.dq_in, bf16[384,128]{1,0:T(8,128)(2,1)S(1)} %get-tuple-element.10.dk_in, bf16[384,128]{1,0:T(8,128)(2,1)S(1)} %get-tuple-element.11.dv_in), custom_call_target="tpu_custom_call" | custom-call | tf_op jit(solution)/shard_map/put_out/pallas_call | solution.py:417

commit v4 on v3

--- a/solution.py
+++ b/solution.py
@@ -84,9 +84,6 @@
         pltpu.make_async_copy(assist_hbm, assist, in_sem.at[4]),
         pltpu.make_async_copy(first_hbm, first, in_sem.at[5]),
     ]
-    for copy in local:
-        copy.start()
-
     def halo_copy(array, block, window, away, slot):
         src = (k_hbm, v_hbm)[array].at[pl.ds(block * BLK, BLK)]
         dst = (win_k, win_v)[array].at[pl.ds(window * BLK, BLK)]
@@ -105,7 +102,7 @@
         block = NB - 1 if window == 0 else window - 1
         for array in (0, 1):
             halo_copies.append(
-                (away, window, halo_copy(array, block, window, away, 2 * window + array))
+                (away, window, array, halo_copy(array, block, window, away, 2 * window + array))
             )
 
     def back_copy(array, window, slot):
@@ -128,7 +125,8 @@
     for window in (0, 1, 2, 3):
         away = 2 if window == 0 else 1
         for array in (0, 1):
-            back_copies.append((away, window, back_copy(array, window, 2 * window + array)))
+            slot = 2 * window + array
+            back_copies.append((away, window, array, back_copy(array, window, slot)))
 
     barrier = pltpu.get_barrier_semaphore()
     for away in (1, 2):
@@ -143,13 +141,16 @@
     def _():
         pl.semaphore_wait(barrier, jnp.minimum(ranks - 1 - me, 2))
 
-    for away, window, copy in halo_copies:
+    for away, window, array, copy in halo_copies:
 
         @pl.when(me + away < ranks)
         def _():
             copy.start()
 
-    for away, window, _ in halo_copies[::2]:
+    for copy in local:
+        copy.start()
+
+    for away, window, _, _ in halo_copies[::2]:
 
         @pl.when(me < away)
         def _():
@@ -157,7 +158,7 @@
             win_k[window * BLK : (window + 1) * BLK, :] = zero
             win_v[window * BLK : (window + 1) * BLK, :] = zero
 
-    for away, window, _ in back_copies[::2]:
+    for away, window, _, _ in back_copies[::2]:
 
         @pl.when(me + away >= ranks)
         def _():
@@ -235,11 +236,16 @@
             finished[unit] = normalise(unit)
         return finished[unit]
 
+    def inverse_of(unit):
+        total = jnp.sum(l_buf[unit], axis=0, keepdims=True)
+        return jnp.where(total > 0.0, 1.0 / total, 0.0)
+
+    def delta_of(unit, inverse):
+        return jnp.sum(e_buf[unit], axis=0, keepdims=True) * inverse
+
     def normalise(unit):
-        total = jnp.sum(l_buf[unit], axis=0, keepdims=True)
-        total_e = jnp.sum(e_buf[unit], axis=0, keepdims=True)
-        inverse = jnp.where(total > 0.0, 1.0 / total, 0.0)
-        return inverse, total_e * inverse
+        inverse = inverse_of(unit)
+        return inverse, delta_of(unit, inverse)
 
     written = set()
 
@@ -263,21 +269,23 @@
                 acc_k[keys, :] = part_k
                 acc_v[keys, :] = part_v
 
-    def received(copies, windows):
-        for away, window, copy in copies:
-            if window in windows:
+    def received(copies, windows, arrays):
+        for away, window, array, copy in copies:
+            if window in windows and array in arrays:
 
                 @pl.when(me >= away)
                 def _():
                     copy.wait_recv()
 
-    def give_back(windows):
+    def give_back(windows, arrays):
         for window in windows:
             keys = slice(window * BLK, (window + 1) * BLK)
-            out_k[keys, :] = (acc_k[keys, :] * scale).astype(BF16)
-            out_v[keys, :] = acc_v[keys, :].astype(BF16)
-        for away, window, copy in back_copies:
-            if window in windows:
+            if 0 in arrays:
+                out_k[keys, :] = (acc_k[keys, :] * scale).astype(BF16)
+            if 1 in arrays:
+                out_v[keys, :] = acc_v[keys, :].astype(BF16)
+        for away, window, array, copy in back_copies:
+            if window in windows and array in arrays:
 
                 @pl.when(me >= away)
                 def _():
@@ -285,15 +293,66 @@
 
     weigh(0, (4, 5), True)
     weigh(1, (4, 5, 6), True)
-    received(halo_copies, (1, 2, 3))
+    received(halo_copies, (1, 2, 3), (0, 1))
     weigh(1, (1, 2, 3), False)
     weigh(0, (1, 2, 3), False)
     grads(1, (1, 2, 3))
-    received(halo_copies, (0,))
-    weigh(0, (0,), False)
-    for windows in ((1,), (2,), (3,), (0,)):
-        grads(0, windows)
-        give_back(windows)
+
+    far = slice(0, BLK)
+    units = range(UNITS)
+    received(halo_copies, (0,), (0,))
+    for unit in units:
+        at = slice(unit * UNIT, (unit + 1) * UNIT)
+        w = jnp.exp2(dot_nt(win_k[far, :], q_all[at, :]) * (scale * math.log2(math.e)))
+        w_buf[unit, far, :] = w
+        l_buf[unit] = l_buf[unit] + valid(0, 0) * sub_sum(w)
+    inverses = [inverse_of(unit) for unit in units]
+
+    def add(acc, window, part):
+        keys = slice(window * BLK, (window + 1) * BLK)
+        acc[keys, :] = part if window == 0 else acc[keys, :] + part
+
+    def value_grads(window):
+        keys = slice(window * BLK, (window + 1) * BLK)
+        part = None
+        for unit in units:
+            at = slice(unit * UNIT, (unit + 1) * UNIT)
+            attention = w_buf[unit, keys, :] * (inverses[unit] * valid(0, window))
+            more = dot_nn(attention.astype(BF16), g_all[at, :])
+            part = more if part is None else part + more
+        add(acc_v, window, part)
+
+    def key_grads(window):
+        keys = slice(window * BLK, (window + 1) * BLK)
+        part = None
+        for unit in units:
+            at = slice(unit * UNIT, (unit + 1) * UNIT)
+            attention = w_buf[unit, keys, :] * (inverses[unit] * valid(0, window))
+            score_grad = (attention * (d_buf[unit, keys, :] - deltas[unit])).astype(BF16)
+            ds_buf[unit, keys, :] = score_grad
+            more = dot_nn(score_grad, q_all[at, :])
+            part = more if part is None else part + more
+        add(acc_k, window, part)
+
+    for window in (1, 2, 3):
+        value_grads(window)
+        give_back((window,), (1,))
+    received(halo_copies, (0,), (1,))
+    for unit in units:
+        at = slice(unit * UNIT, (unit + 1) * UNIT)
+        prob_grad = dot_nt(win_v[far, :], g_all[at, :])
+        d_buf[unit, far, :] = prob_grad
+        e_buf[unit] = e_buf[unit] + valid(0, 0) * sub_sum(w_buf[unit, far, :] * prob_grad)
+    deltas = [delta_of(unit, inverses[unit]) for unit in units]
+    for window in (1, 2, 3):
+        key_grads(window)
+        give_back((window,), (0,))
+    value_grads(0)
+    key_grads(0)
+    give_back((0,), (0, 1))
+    for unit in units:
+        finished[unit] = (inverses[unit], deltas[unit])
+    written.add(0)
 
     for window in range(WIN):
         keys = slice(window * BLK, (window + 1) * BLK)
@@ -316,7 +375,7 @@
                 dq_out[BLK : 2 * BLK, cols] = jnp.where(take, both, middle)
                 dq_out[2 * BLK :, cols] = jnp.where(is_low, zero, both)
 
-    for away, window, copy in back_copies:
+    for away, window, array, copy in back_copies:
 
         @pl.when(me + away < ranks)
         def _():
@@ -330,13 +389,13 @@
     dk_out[last:, :] = (total_k[last:] + far_k[...].astype(F32)).astype(BF16)
     dv_out[last:, :] = (total_v[last:] + far_v[...].astype(F32)).astype(BF16)
 
-    for away, window, copy in halo_copies:
+    for away, window, array, copy in halo_copies:
 
         @pl.when(me + away < ranks)
         def _():
             copy.wait_send()
 
-    for away, window, copy in back_copies:
+    for away, window, array, copy in back_copies:
 
         @pl.when(me >= away)
         def _():

time: 25 us -> 24.6 us (0.984)
  Pallas kernels: 24.2 us -> 23.8 us
    pallas_call x1, Pallas kernels: 23.3 us -> 22.8 us  [per_device(): pl.pallas_call(body, out_shape=shapes, in_specs=[hbm, hbm, hbm, hbm, hbm,...]
where the time goes in v4:
time: 24.6 us; the launch traced here: 24.4 us
  Pallas kernels  23.8 us (97%)
  between operations  0.64 us (3%)
    pallas_call x1, Pallas kernels, per_device(): pl.pallas_call(body, out_shape=shapes, in_specs=[hbm, hbm, hbm, hbm, hbm,...  22.8 us
    pallas_call x1, Pallas kernels, per_device(): pl.pallas_call(put_out, out_shape=shapes, in_specs=[vmem, vmem, vmem], ou...  0.96 us

profile of v4, /device:TPU:1, one launch (start us, length us, event | category | flops | bytes accessed | tf_op | source)
XLA Modules:
  0.0 24.4 jit_solution(2230891553559389224)
XLA Ops:
  0.6 22.8 %attention_backward.1 = (bf16[384,1024]{1,0:T(8,128)(2,1)S(1)}, bf16[384,128]{1,0:T(8,128)(2,1)S(1)}, bf16[384,128]{1,0:T(8,128)(2,1)S(1)}) custom-call(s32[1,48]{1,0:T(1,128)} %refs_0_.1, s32[1,48]{1,0:T(1,128)} %refs_1_.1, bf16[384,1024]{1,0:T(8,128)(2,1)} %bitcast.7, bf16[384,128]{1,0:T(8,128)(2,1)} %bitcast.9, bf16[384,128]{1,0:T(8,128)(2,1)} %bitcast.10, ...), custom_call_target="tpu_custom_call" | custom-call | tf_op jit(solution)/shard_map/attention_backward/pallas_call | solution.py:465
  23.5 1.0 %put_out.1 = (bf16[384,1024]{1,0:T(8,128)(2,1)}, bf16[384,128]{1,0:T(8,128)(2,1)}, bf16[384,128]{1,0:T(8,128)(2,1)}) custom-call(bf16[384,1024]{1,0:T(8,128)(2,1)S(1)} %get-tuple-element.9.dq_in, bf16[384,128]{1,0:T(8,128)(2,1)S(1)} %get-tuple-element.10.dk_in, bf16[384,128]{1,0:T(8,128)(2,1)S(1)} %get-tuple-element.11.dv_in), custom_call_target="tpu_custom_call" | custom-call | tf_op jit(solution)/shard_map/put_out/pallas_call | solution.py:476

commit v5 on v3

--- a/solution.py
+++ b/solution.py
@@ -61,8 +61,10 @@
     out_v,
     near_k,
     near_v,
-    far_k,
-    far_v,
+    q_next,
+    g_next,
+    sum_out,
+    sum_in,
     assist,
     first,
     in_sem,
@@ -70,6 +72,9 @@
     fr_sem,
     bs_sem,
     br_sem,
+    ns_sem,
+    nr_sem,
+    here_sem,
 ):
     me = lax.axis_index("ctx")
     scale = 1.0 / math.sqrt(BLK)
@@ -84,9 +89,6 @@
         pltpu.make_async_copy(assist_hbm, assist, in_sem.at[4]),
         pltpu.make_async_copy(first_hbm, first, in_sem.at[5]),
     ]
-    for copy in local:
-        copy.start()
-
     def halo_copy(array, block, window, away, slot):
         src = (k_hbm, v_hbm)[array].at[pl.ds(block * BLK, BLK)]
         dst = (win_k, win_v)[array].at[pl.ds(window * BLK, BLK)]
@@ -105,30 +107,41 @@
         block = NB - 1 if window == 0 else window - 1
         for array in (0, 1):
             halo_copies.append(
-                (away, window, halo_copy(array, block, window, away, 2 * window + array))
+                (away, window, array, halo_copy(array, block, window, away, 2 * window + array))
             )
 
-    def back_copy(array, window, slot):
-        src = (out_k, out_v)[array].at[pl.ds(window * BLK, BLK)]
-        if window == 0:
-            dst = (far_k, far_v)[array]
-        else:
-            dst = (near_k, near_v)[array].at[pl.ds((window - 1) * BLK, BLK)]
-        away = 2 if window == 0 else 1
-        return pltpu.make_async_remote_copy(
-            src_ref=src,
-            dst_ref=dst,
-            send_sem=bs_sem.at[slot],
-            recv_sem=br_sem.at[slot],
-            device_id={"ctx": me - away},
-            device_id_type=MESH,
+    back_copies = []
+    for window in (1, 2, 3):
+        for array in (0, 1):
+            slot = 2 * (window - 1) + array
+            copy = pltpu.make_async_remote_copy(
+                src_ref=(out_k, out_v)[array].at[pl.ds(window * BLK, BLK)],
+                dst_ref=(near_k, near_v)[array].at[pl.ds((window - 1) * BLK, BLK)],
+                send_sem=bs_sem.at[slot],
+                recv_sem=br_sem.at[slot],
+                device_id={"ctx": me - 1},
+                device_id_type=MESH,
+            )
+            back_copies.append((1, window, array, copy))
+
+    lent = []
+    for slot, (src, dst) in enumerate(
+        (
+            (q_hbm.at[pl.ds(0, BLK)], q_next),
+            (g_hbm.at[pl.ds(0, BLK)], g_next),
+            (sum_out, sum_in),
         )
-
-    back_copies = []
-    for window in (0, 1, 2, 3):
-        away = 2 if window == 0 else 1
-        for array in (0, 1):
-            back_copies.append((away, window, back_copy(array, window, 2 * window + array)))
+    ):
+        lent.append(
+            pltpu.make_async_remote_copy(
+                src_ref=src,
+                dst_ref=dst,
+                send_sem=ns_sem.at[slot],
+                recv_sem=nr_sem.at[slot],
+                device_id={"ctx": me - 1},
+                device_id_type=MESH,
+            )
+        )
 
     barrier = pltpu.get_barrier_semaphore()
     for away in (1, 2):
@@ -142,14 +155,20 @@
     @pl.when(me < ranks - 1)
     def _():
         pl.semaphore_wait(barrier, jnp.minimum(ranks - 1 - me, 2))
-
-    for away, window, copy in halo_copies:
+        pl.semaphore_signal(
+            here_sem, inc=1, device_id={"ctx": me + 1}, device_id_type=MESH
+        )
+
+    for away, window, array, copy in halo_copies:
 
         @pl.when(me + away < ranks)
         def _():
             copy.start()
 
-    for away, window, _ in halo_copies[::2]:
+    for copy in local:
+        copy.start()
+
+    for away, window, _, _ in halo_copies[::2]:
 
         @pl.when(me < away)
         def _():
@@ -157,33 +176,32 @@
             win_k[window * BLK : (window + 1) * BLK, :] = zero
             win_v[window * BLK : (window + 1) * BLK, :] = zero
 
-    for away, window, _ in back_copies[::2]:
-
-        @pl.when(me + away >= ranks)
-        def _():
-            zero = jnp.zeros((BLK, BLK), BF16)
-            if window == 0:
-                far_k[...] = zero
-                far_v[...] = zero
-            else:
-                near_k[(window - 1) * BLK : window * BLK, :] = zero
-                near_v[(window - 1) * BLK : window * BLK, :] = zero
+    @pl.when(me == ranks - 1)
+    def _():
+        near_k[...] = jnp.zeros_like(near_k)
+        near_v[...] = jnp.zeros_like(near_v)
+        q_next[...] = jnp.zeros_like(q_next)
+        g_next[...] = jnp.zeros_like(g_next)
+        sum_in[...] = jnp.zeros_like(sum_in)
 
     for copy in local:
         copy.wait()
 
-    mark = [assist[0, base + i] for i in range(NB)]
-    turn = [first[0, base + i] for i in range(NB)]
+    after = jnp.minimum(base + NB, ranks * NB - 1)
+    mark = [assist[0, base + i] for i in range(NB)] + [assist[0, after]]
+    turn = [first[0, base + i] for i in range(NB)] + [first[0, after]]
     head_is_first = mark[0] == 1
     tail_is_last = mark[2] == 1
     slot_block = (jnp.where(head_is_first, 0, 1), jnp.where(tail_is_last, 2, 1))
     slot_turn = (
         jnp.where(head_is_first, turn[0], turn[1]),
         jnp.where(tail_is_last, turn[2], turn[1]),
+        turn[3],
     )
     slot_live = (
         jnp.maximum(mark[0], mark[1]),
         jnp.maximum(mark[2], mark[0] * mark[1]),
+        jnp.where(me < ranks - 1, mark[3], 0),
     )
 
     def valid(slot, window):
@@ -216,44 +234,44 @@
                 scores = dot_nt(win_k[keys, :], q_t)
                 prob_grad = dot_nt(win_v[keys, :], g_t)
                 w = jnp.exp2(scores * (scale * math.log2(math.e)))
-                if window >= REACH:
+                if window >= REACH and slot < 2:
                     w = jnp.where(ahead >= (window - REACH - slot_block[slot]) * BLK, w, 0.0)
                 w_buf[unit, keys, :] = w
                 d_buf[unit, keys, :] = prob_grad
                 on = valid(slot, window)
                 more = on * sub_sum(w)
                 more_e = on * sub_sum(w * prob_grad)
+                if slot == 0 and window == REACH:
+                    sum_out[0, unit] = more
+                    sum_out[1, unit] = more_e
                 total = more if total is None else total + more
                 total_e = more_e if total_e is None else total_e + more_e
             l_buf[unit] = total
             e_buf[unit] = total_e
 
-    finished = {}
-
-    def finish(unit):
-        if unit not in finished:
-            finished[unit] = normalise(unit)
-        return finished[unit]
-
-    def normalise(unit):
-        total = jnp.sum(l_buf[unit], axis=0, keepdims=True)
-        total_e = jnp.sum(e_buf[unit], axis=0, keepdims=True)
+    def normalise(unit, lent_sums=None):
+        total, total_e = l_buf[unit], e_buf[unit]
+        if lent_sums is not None:
+            total, total_e = total + lent_sums[0], total_e + lent_sums[1]
+        total = jnp.sum(total, axis=0, keepdims=True)
         inverse = jnp.where(total > 0.0, 1.0 / total, 0.0)
-        return inverse, total_e * inverse
+        return inverse, jnp.sum(total_e, axis=0, keepdims=True) * inverse
 
     written = set()
 
-    def grads(slot, windows):
-        for unit in range(slot * UNITS, (slot + 1) * UNITS):
+    def grads(slot, windows, stats, factor=1.0, keep=True):
+        for u in range(UNITS):
+            unit = slot * UNITS + u
             at = slice(unit * UNIT, (unit + 1) * UNIT)
             q_t = q_all[at, :]
             g_t = g_all[at, :]
-            inverse, delta = finish(unit)
+            inverse, delta = stats[u]
             for window in windows:
                 keys = slice(window * BLK, (window + 1) * BLK)
-                attention = w_buf[unit, keys, :] * (inverse * valid(slot, window))
+                attention = w_buf[unit, keys, :] * (inverse * (valid(slot, window) * factor))
                 score_grad = (attention * (d_buf[unit, keys, :] - delta)).astype(BF16)
-                ds_buf[unit, keys, :] = score_grad
+                if keep:
+                    ds_buf[unit, keys, :] = score_grad
                 part_k = dot_nn(score_grad, q_t)
                 part_v = dot_nn(attention.astype(BF16), g_t)
                 if window in written:
@@ -263,9 +281,9 @@
                 acc_k[keys, :] = part_k
                 acc_v[keys, :] = part_v
 
-    def received(copies, windows):
-        for away, window, copy in copies:
-            if window in windows:
+    def received(copies, windows, arrays):
+        for away, window, array, copy in copies:
+            if window in windows and array in arrays:
 
                 @pl.when(me >= away)
                 def _():
@@ -276,7 +294,7 @@
             keys = slice(window * BLK, (window + 1) * BLK)
             out_k[keys, :] = (acc_k[keys, :] * scale).astype(BF16)
             out_v[keys, :] = acc_v[keys, :].astype(BF16)
-        for away, window, copy in back_copies:
+        for away, window, array, copy in back_copies:
             if window in windows:
 
                 @pl.when(me >= away)
@@ -285,22 +303,58 @@
 
     weigh(0, (4, 5), True)
     weigh(1, (4, 5, 6), True)
-    received(halo_copies, (1, 2, 3))
+
+    @pl.when(me >= 1)
+    def _():
+        pl.semaphore_wait(here_sem, 1)
+        for copy in lent:
+            copy.start()
+
+    @pl.when(me < ranks - 1)
+    def _():
+        for copy in lent:
+            copy.wait_recv()
+
+    for head in range(QH):
+        at = slice(2 * SLOT + head * BLK, 2 * SLOT + (head + 1) * BLK)
+        cols = slice(head * BLK, (head + 1) * BLK)
+        q_all[at, :] = q_next[:, cols]
+        g_all[at, :] = g_next[:, cols]
+    weigh(2, (4, 5, 6), True)
+
+    received(halo_copies, (1, 2, 3), (0, 1))
     weigh(1, (1, 2, 3), False)
     weigh(0, (1, 2, 3), False)
-    grads(1, (1, 2, 3))
-    received(halo_copies, (0,))
+    weigh(2, (3,), False)
+    stats = [normalise(UNITS + u) for u in range(UNITS)]
+    grads(1, (1, 2, 3), stats)
+    near_stats = [normalise(u) for u in range(UNITS)]
+    not_lent = jnp.where(head_is_first, jnp.float32(0.0), jnp.float32(1.0))
+    grads(0, (1, 2, 3), near_stats, not_lent, False)
+    next_stats = [
+        normalise(2 * UNITS + u, (sum_in[0, u], sum_in[1, u])) for u in range(UNITS)
+    ]
+    grads(2, (3,), next_stats, 1.0, False)
+    give_back((1, 2, 3))
+    grads(2, (4, 5, 6), next_stats, 1.0, False)
+    grads(1, (4, 5, 6), stats)
+
+    received(halo_copies, (0,), (0, 1))
     weigh(0, (0,), False)
-    for windows in ((1,), (2,), (3,), (0,)):
-        grads(0, windows)
-        give_back(windows)
+    full_stats = [normalise(u) for u in range(UNITS)]
+    for u in range(UNITS):
+        inverse, delta = full_stats[u]
+        for window in (0, 1, 2, 3):
+            keys = slice(window * BLK, (window + 1) * BLK)
+            attention = w_buf[u, keys, :] * (inverse * valid(0, window))
+            ds_buf[u, keys, :] = (attention * (d_buf[u, keys, :] - delta)).astype(BF16)
+    grads(0, (4, 5), full_stats)
 
     for window in range(WIN):
         keys = slice(window * BLK, (window + 1) * BLK)
         k_t[:, keys] = win_k[keys, :].T
     zero = jnp.zeros((), BF16)
-    for slot, windows in ((0, (4, 5)), (1, (4, 5, 6))):
-        grads(slot, windows)
+    for slot in (0, 1):
         keys = slice(slot * BLK, (slot + WIN - 1) * BLK)
         for u in range(UNITS):
             part = dot_nn(k_t[:, keys], ds_buf[slot * UNITS + u, keys, :]) * scale
@@ -316,31 +370,31 @@
                 dq_out[BLK : 2 * BLK, cols] = jnp.where(take, both, middle)
                 dq_out[2 * BLK :, cols] = jnp.where(is_low, zero, both)
 
-    for away, window, copy in back_copies:
+    for away, window, array, copy in halo_copies:
+
+        @pl.when(me + away < ranks)
+        def _():
+            copy.wait_send()
+
+    for away, window, array, copy in back_copies:
+
+        @pl.when(me >= away)
+        def _():
+            copy.wait_send()
+
+    @pl.when(me >= 1)
+    def _():
+        for copy in lent:
+            copy.wait_send()
+
+    for away, window, array, copy in back_copies:
 
         @pl.when(me + away < ranks)
         def _():
             copy.wait_recv()
 
-    total_k = acc_k[halo:, :] * scale + near_k[...].astype(F32)
-    total_v = acc_v[halo:, :] + near_v[...].astype(F32)
-    last = (NB - 1) * BLK
-    dk_out[:last, :] = total_k[:last].astype(BF16)
-    dv_out[:last, :] = total_v[:last].astype(BF16)
-    dk_out[last:, :] = (total_k[last:] + far_k[...].astype(F32)).astype(BF16)
-    dv_out[last:, :] = (total_v[last:] + far_v[...].astype(F32)).astype(BF16)
-
-    for away, window, copy in halo_copies:
-
-        @pl.when(me + away < ranks)
-        def _():
-            copy.wait_send()
-
-    for away, window, copy in back_copies:
-
-        @pl.when(me >= away)
-        def _():
-            copy.wait_send()
+    dk_out[...] = (acc_k[halo:, :] * scale + near_k[...].astype(F32)).astype(BF16)
+    dv_out[...] = (acc_v[halo:, :] + near_v[...].astype(F32)).astype(BF16)
 
 
 def put_out(dq_in, dk_in, dv_in, dq_hbm, dk_hbm, dv_hbm, sem):
@@ -359,18 +413,18 @@
     rows = NB * BLK
     hbm = pl.BlockSpec(memory_space=pltpu.HBM)
     vmem = pl.BlockSpec(memory_space=pltpu.VMEM)
-    units = 2 * UNITS
+    units = 3 * UNITS
     scratch = [
         pltpu.VMEM((rows, SLOT), BF16),
         pltpu.VMEM((rows, SLOT), BF16),
         pltpu.VMEM((WIN * BLK, BLK), BF16),
         pltpu.VMEM((WIN * BLK, BLK), BF16),
-        pltpu.VMEM((2 * SLOT, BLK), BF16),
-        pltpu.VMEM((2 * SLOT, BLK), BF16),
+        pltpu.VMEM((3 * SLOT, BLK), BF16),
+        pltpu.VMEM((3 * SLOT, BLK), BF16),
         pltpu.VMEM((BLK, WIN * BLK), BF16),
         pltpu.VMEM((units, WIN * BLK, UNIT), F32),
         pltpu.VMEM((units, WIN * BLK, UNIT), F32),
-        pltpu.VMEM((units, WIN * BLK, UNIT), BF16),
+        pltpu.VMEM((2 * UNITS, WIN * BLK, UNIT), BF16),
         pltpu.VMEM((units, 8, UNIT), F32),
         pltpu.VMEM((units, 8, UNIT), F32),
         pltpu.VMEM((WIN * BLK, BLK), F32),
@@ -379,15 +433,20 @@
         pltpu.VMEM((REACH * BLK, BLK), BF16),
         pltpu.VMEM((rows, BLK), BF16),
         pltpu.VMEM((rows, BLK), BF16),
-        pltpu.VMEM((BLK, BLK), BF16),
-        pltpu.VMEM((BLK, BLK), BF16),
+        pltpu.VMEM((BLK, SLOT), BF16),
+        pltpu.VMEM((BLK, SLOT), BF16),
+        pltpu.VMEM((2, UNITS, 8, UNIT), F32),
+        pltpu.VMEM((2, UNITS, 8, UNIT), F32),
         pltpu.SMEM((1, assistant.shape[1]), jnp.int32),
         pltpu.SMEM((1, assistant.shape[1]), jnp.int32),
         pltpu.SemaphoreType.DMA((6,)),
         pltpu.SemaphoreType.DMA((8,)),
         pltpu.SemaphoreType.DMA((8,)),
-        pltpu.SemaphoreType.DMA((8,)),
-        pltpu.SemaphoreType.DMA((8,)),
+        pltpu.SemaphoreType.DMA((6,)),
+        pltpu.SemaphoreType.DMA((6,)),
+        pltpu.SemaphoreType.DMA((3,)),
+        pltpu.SemaphoreType.DMA((3,)),
+        pltpu.SemaphoreType.REGULAR,
     ]
 
     blocks = [
@@ -410,7 +469,7 @@
         out_specs=(vmem, vmem, vmem),
         scratch_shapes=scratch,
         compiler_params=pltpu.CompilerParams(
-            collective_id=0, has_side_effects=True, vmem_limit_bytes=40 * 1024 * 1024
+            collective_id=0, has_side_effects=True, vmem_limit_bytes=44 * 1024 * 1024
         ),
         name="attention_backward",
     )(*blocks)

time: 25 us -> 23.4 us (0.936)
  the two profiles are of different devices: /device:TPU:1 before, /device:TPU:547 now
where the time goes in v5:
time: 23.4 us; the launch traced here: 23.2 us
  Pallas kernels  22.6 us (97%)
  between operations  0.64 us (3%)
    pallas_call x1, Pallas kernels, per_device(): pl.pallas_call(body, out_shape=shapes, in_specs=[hbm, hbm, hbm, hbm, hbm,...  21.6 us
    pallas_call x1, Pallas kernels, per_device(): pl.pallas_call(put_out, out_shape=shapes, in_specs=[vmem, vmem, vmem], ou...  0.96 us

profile of v5, /device:TPU:547, one launch (start us, length us, event | category | flops | bytes accessed | tf_op | source)
XLA Modules:
  0.0 23.2 jit_solution(15984321956785881911)
XLA Ops:
  0.6 21.6 %attention_backward.1 = (bf16[384,1024]{1,0:T(8,128)(2,1)S(1)}, bf16[384,128]{1,0:T(8,128)(2,1)S(1)}, bf16[384,128]{1,0:T(8,128)(2,1)S(1)}) custom-call(s32[1,48]{1,0:T(1,128)} %refs_0_.1, s32[1,48]{1,0:T(1,128)} %refs_1_.1, bf16[384,1024]{1,0:T(8,128)(2,1)} %bitcast.7, bf16[384,128]{1,0:T(8,128)(2,1)} %bitcast.9, bf16[384,128]{1,0:T(8,128)(2,1)} %bitcast.10, ...), custom_call_target="tpu_custom_call" | custom-call | tf_op jit(solution)/shard_map/attention_backward/pallas_call | solution.py:465
  22.3 1.0 %put_out.1 = (bf16[384,1024]{1,0:T(8,128)(2,1)}, bf16[384,128]{1,0:T(8,128)(2,1)}, bf16[384,128]{1,0:T(8,128)(2,1)}) custom-call(bf16[384,1024]{1,0:T(8,128)(2,1)S(1)} %get-tuple-element.9.dq_in, bf16[384,128]{1,0:T(8,128)(2,1)S(1)} %get-tuple-element.10.dk_in, bf16[384,128]{1,0:T(8,128)(2,1)S(1)} %get-tuple-element.11.dv_in), custom_call_target="tpu_custom_call" | custom-call | tf_op jit(solution)/shard_map/put_out/pallas_call | solution.py:476

commit v6 on v5

--- a/solution.py
+++ b/solution.py
@@ -168,6 +168,12 @@
     for copy in local:
         copy.start()
 
+    @pl.when((me >= 1) & (me % 2 == 0))
+    def _():
+        pl.semaphore_wait(here_sem, 1)
+        for copy in lent[:2]:
+            copy.start()
+
     for away, window, _, _ in halo_copies[::2]:
 
         @pl.when(me < away)
@@ -242,20 +248,23 @@
                 more = on * sub_sum(w)
                 more_e = on * sub_sum(w * prob_grad)
                 if slot == 0 and window == REACH:
-                    sum_out[0, unit] = more
-                    sum_out[1, unit] = more_e
+                    row = UNITS + unit
+                    sum_out[unit : unit + 1, :] = jnp.sum(more, axis=0, keepdims=True)
+                    sum_out[row : row + 1, :] = jnp.sum(more_e, axis=0, keepdims=True)
                 total = more if total is None else total + more
                 total_e = more_e if total_e is None else total_e + more_e
             l_buf[unit] = total
             e_buf[unit] = total_e
 
-    def normalise(unit, lent_sums=None):
-        total, total_e = l_buf[unit], e_buf[unit]
-        if lent_sums is not None:
-            total, total_e = total + lent_sums[0], total_e + lent_sums[1]
-        total = jnp.sum(total, axis=0, keepdims=True)
+    def normalise(unit, lent_row=None):
+        total = jnp.sum(l_buf[unit], axis=0, keepdims=True)
+        total_e = jnp.sum(e_buf[unit], axis=0, keepdims=True)
+        if lent_row is not None:
+            row = UNITS + lent_row
+            total = total + sum_in[lent_row : lent_row + 1, :]
+            total_e = total_e + sum_in[row : row + 1, :]
         inverse = jnp.where(total > 0.0, 1.0 / total, 0.0)
-        return inverse, jnp.sum(total_e, axis=0, keepdims=True) * inverse
+        return inverse, total_e * inverse
 
     written = set()
 
@@ -304,11 +313,15 @@
     weigh(0, (4, 5), True)
     weigh(1, (4, 5, 6), True)
 
+    @pl.when(me % 2 == 1)
+    def _():
+        pl.semaphore_wait(here_sem, 1)
+        for copy in lent[:2]:
+            copy.start()
+
     @pl.when(me >= 1)
     def _():
-        pl.semaphore_wait(here_sem, 1)
-        for copy in lent:
-            copy.start()
+        lent[2].start()
 
     @pl.when(me < ranks - 1)
     def _():
@@ -331,9 +344,7 @@
     near_stats = [normalise(u) for u in range(UNITS)]
     not_lent = jnp.where(head_is_first, jnp.float32(0.0), jnp.float32(1.0))
     grads(0, (1, 2, 3), near_stats, not_lent, False)
-    next_stats = [
-        normalise(2 * UNITS + u, (sum_in[0, u], sum_in[1, u])) for u in range(UNITS)
-    ]
+    next_stats = [normalise(2 * UNITS + u, u) for u in range(UNITS)]
     grads(2, (3,), next_stats, 1.0, False)
     give_back((1, 2, 3))
     grads(2, (4, 5, 6), next_stats, 1.0, False)
@@ -435,8 +446,8 @@
         pltpu.VMEM((rows, BLK), BF16),
         pltpu.VMEM((BLK, SLOT), BF16),
         pltpu.VMEM((BLK, SLOT), BF16),
-        pltpu.VMEM((2, UNITS, 8, UNIT), F32),
-        pltpu.VMEM((2, UNITS, 8, UNIT), F32),
+        pltpu.VMEM((2 * UNITS, UNIT), F32),
+        pltpu.VMEM((2 * UNITS, UNIT), F32),
         pltpu.SMEM((1, assistant.shape[1]), jnp.int32),
         pltpu.SMEM((1, assistant.shape[1]), jnp.int32),
         pltpu.SemaphoreType.DMA((6,)),

time: 23.4 us -> 22.9 us (0.979)
  the two profiles are of different devices: /device:TPU:547 before, /device:TPU:1 now
where the time goes in v6:
time: 22.9 us; the launch traced here: 22.7 us
  Pallas kernels  22.1 us (97%)
  between operations  0.64 us (3%)
    pallas_call x1, Pallas kernels, per_device(): pl.pallas_call(body, out_shape=shapes, in_specs=[hbm, hbm, hbm, hbm, hbm,...  21.1 us
    pallas_call x1, Pallas kernels, per_device(): pl.pallas_call(put_out, out_shape=shapes, in_specs=[vmem, vmem, vmem], ou...  0.96 us

profile of v6, /device:TPU:1, one launch (start us, length us, event | category | flops | bytes accessed | tf_op | source)
XLA Modules:
  0.0 22.7 jit_solution(12589875625829552547)
XLA Ops:
  0.6 21.1 %attention_backward.1 = (bf16[384,1024]{1,0:T(8,128)(2,1)S(1)}, bf16[384,128]{1,0:T(8,128)(2,1)S(1)}, bf16[384,128]{1,0:T(8,128)(2,1)S(1)}) custom-call(s32[1,48]{1,0:T(1,128)} %refs_0_.1, s32[1,48]{1,0:T(1,128)} %refs_1_.1, bf16[384,1024]{1,0:T(8,128)(2,1)} %bitcast.7, bf16[384,128]{1,0:T(8,128)(2,1)} %bitcast.9, bf16[384,128]{1,0:T(8,128)(2,1)} %bitcast.10, ...), custom_call_target="tpu_custom_call" | custom-call | tf_op jit(solution)/shard_map/attention_backward/pallas_call | solution.py:476
  21.8 1.0 %put_out.1 = (bf16[384,1024]{1,0:T(8,128)(2,1)}, bf16[384,128]{1,0:T(8,128)(2,1)}, bf16[384,128]{1,0:T(8,128)(2,1)}) custom-call(bf16[384,1024]{1,0:T(8,128)(2,1)S(1)} %get-tuple-element.9.dq_in, bf16[384,128]{1,0:T(8,128)(2,1)S(1)} %get-tuple-element.10.dk_in, bf16[384,128]{1,0:T(8,128)(2,1)S(1)} %get-tuple-element.11.dv_in), custom_call_target="tpu_custom_call" | custom-call | tf_op jit(solution)/shard_map/put_out/pallas_call | solution.py:487

commit v7 on v6

--- a/solution.py
+++ b/solution.py
@@ -346,9 +346,9 @@
     grads(0, (1, 2, 3), near_stats, not_lent, False)
     next_stats = [normalise(2 * UNITS + u, u) for u in range(UNITS)]
     grads(2, (3,), next_stats, 1.0, False)
-    give_back((1, 2, 3))
     grads(2, (4, 5, 6), next_stats, 1.0, False)
     grads(1, (4, 5, 6), stats)
+    give_back((1, 2, 3))
 
     received(halo_copies, (0,), (0, 1))
     weigh(0, (0,), False)

time: 22.9 us -> 23 us (level)
  no operation moved by 1% of the time
where the time goes in v7:
time: 23 us; the launch traced here: 22.8 us
  Pallas kernels  22.1 us (96%)
  between operations  0.64 us (3%)
    pallas_call x1, Pallas kernels, per_device(): pl.pallas_call(body, out_shape=shapes, in_specs=[hbm, hbm, hbm, hbm, hbm,...  21.2 us
    pallas_call x1, Pallas kernels, per_device(): pl.pallas_call(put_out, out_shape=shapes, in_specs=[vmem, vmem, vmem], ou...  0.96 us

profile of v7, /device:TPU:1, one launch (start us, length us, event | category | flops | bytes accessed | tf_op | source)
XLA Modules:
  0.0 22.8 jit_solution(97403753514377462)
XLA Ops:
  0.6 21.2 %attention_backward.1 = (bf16[384,1024]{1,0:T(8,128)(2,1)S(1)}, bf16[384,128]{1,0:T(8,128)(2,1)S(1)}, bf16[384,128]{1,0:T(8,128)(2,1)S(1)}) custom-call(s32[1,48]{1,0:T(1,128)} %refs_0_.1, s32[1,48]{1,0:T(1,128)} %refs_1_.1, bf16[384,1024]{1,0:T(8,128)(2,1)} %bitcast.7, bf16[384,128]{1,0:T(8,128)(2,1)} %bitcast.9, bf16[384,128]{1,0:T(8,128)(2,1)} %bitcast.10, ...), custom_call_target="tpu_custom_call" | custom-call | tf_op jit(solution)/shard_map/attention_backward/pallas_call | solution.py:476
  21.8 1.0 %put_out.1 = (bf16[384,1024]{1,0:T(8,128)(2,1)}, bf16[384,128]{1,0:T(8,128)(2,1)}, bf16[384,128]{1,0:T(8,128)(2,1)}) custom-call(bf16[384,1024]{1,0:T(8,128)(2,1)S(1)} %get-tuple-element.9.dq_in, bf16[384,128]{1,0:T(8,128)(2,1)S(1)} %get-tuple-element.10.dk_in, bf16[384,128]{1,0:T(8,128)(2,1)S(1)} %get-tuple-element.11.dv_in), custom_call_target="tpu_custom_call" | custom-call | tf_op jit(solution)/shard_map/put_out/pallas_call | solution.py:487
